TPU v7x, 32 devices: a whole 2x2x4 slice. The times are simulated.
32 devices in a mesh: rel: 4 (over z), dev: 8 (over y, x, core).
Axes of the slice: x: 2, y: 2, z: 4, core: 2. Of those that a mesh axis runs over, the one named last changes fastest.
Arguments:
- src_feat: bfloat16 [4, 2048, 1024], P('rel', 'dev'), may hold values from -6 to 6
- rel_w_in: bfloat16 [4, 1024, 1024], P('rel', 'dev'), may hold values from -0.1875 to 0.1875
- rel_w_out: bfloat16 [4, 1024, 1024], P('rel', 'dev'), may hold values from -0.1875 to 0.1875
- tile_source: int32 [4, 32], P('rel'), may hold values from 0 to 15
- tile_edges: int32 [4, 32, 128], P('rel'), may hold values from 0 to 16383
- tile_count: int32 [4, 32], P('rel'), may hold values from 0 to 128, as said below
- target_feat: bfloat16 [1024, 1024], P(('dev', 'rel')), may hold values from -6 to 6
- norm_gain: float32 [1024], replicated, may hold values from 0.5 to 2
- tgt_w_in: bfloat16 [1024, 2048], P(None, 'rel'), may hold values from -0.1875 to 0.1875
- tgt_w_out: bfloat16 [2048, 1024], P('rel'), may hold values from -0.125 to 0.125
- out_grad: bfloat16 [1024, 1024], P(('dev', 'rel')), may hold values from -6 to 6
Outputs:
- updated: bfloat16 [1024, 1024], P(('dev', 'rel'))
- src_grad: bfloat16 [4, 2048, 1024], P('rel', 'dev')
Inputs may be any that keep to these rules, and one draw needn't show every extreme that they name: Tile k of a relation joins target rows 128 * (k // 4) onward with source rows 128 * tile_source onward. `tile_edges`: each entry is t * 128 + s for an edge from in-tile source offset s to in-tile target offset t; entries past a tile's count are ignored; the same edge may stand several times. The first tile_count entries of a tile's row of tile_edges are its edges; 0 marks an empty tile; in every relation some tile holds 128 edges.
All inputs are finite; a program needn't handle non-finite values.
Results may differ from a plain program's by a relative error of at most 0.013.
Values may be sent and summed in bfloat16 or wider, within the bound.
No kernel may reach another device: no remote copies, remote signals or barrier semaphores. Data moves between devices by JAX's collectives and lax.ppermute only.
A program may use at most 64 MiB of HBM per device.

v0:
```python
import jax
import jax.numpy as jnp
from jax import lax
from jax.sharding import PartitionSpec as P

TILE = 128
TILE_ROW = 4


eps_norm = 1e-06


def silu_slope(values):
    sigma = jax.nn.sigmoid(values)
    return sigma * (1.0 + values * (1.0 - sigma))


def tile_counts(edge_codes, live_counts):
    live_mask = lax.broadcasted_iota(jnp.int32, edge_codes.shape, 1) < live_counts[:, None]
    lattice = lax.broadcasted_iota(jnp.int32, (1, 1, TILE), 2)
    target_hot = (((edge_codes // TILE)[:, :, None] == lattice) & live_mask[:, :, None]).astype(
        jnp.bfloat16
    )
    source_hot = ((edge_codes % TILE)[:, :, None] == lattice).astype(jnp.bfloat16)
    counts = jnp.einsum("kes,ket->kst", source_hot, target_hot, preferred_element_type=jnp.float32)
    return counts.astype(jnp.bfloat16)


def aggregate(features, source_ids, all_counts):
    breadth = features.shape[0]
    source_total = features.shape[1]
    block_count = source_ids.shape[0] // TILE_ROW
    per_turn = 8 * TILE_ROW
    source_blocks = features.reshape(breadth, source_total // TILE, TILE)

    def aggregate_advance(iteration, running):
        offset = iteration * per_turn
        chosen = lax.dynamic_slice_in_dim(source_ids, offset, per_turn, 0)
        counts = lax.dynamic_slice_in_dim(all_counts, offset, per_turn, 0).reshape(
            8, TILE_ROW, TILE, TILE
        )
        picked = jnp.take(source_blocks, chosen, axis=1).reshape(breadth, 8, TILE_ROW, TILE)
        contrib = jnp.einsum("fbjs,bjst->fbt", picked, counts, preferred_element_type=jnp.float32)
        return lax.dynamic_update_slice_in_dim(
            running, contrib.reshape(breadth, 8 * TILE), iteration * 8 * TILE, 1
        )

    running = jnp.zeros((breadth, block_count * TILE), jnp.float32)
    return lax.fori_loop(0, block_count // 8, aggregate_advance, running)


def spread(grad_targets, source_ids, all_counts, source_total):
    breadth = grad_targets.shape[0]
    block_count = source_ids.shape[0] // TILE_ROW
    per_turn = 8 * TILE_ROW
    source_blocks = source_total // TILE
    target_blocks = grad_targets.reshape(breadth, block_count, TILE)

    def spread_advance(iteration, running):
        offset = iteration * per_turn
        chosen = lax.dynamic_slice_in_dim(source_ids, offset, per_turn, 0)
        counts = lax.dynamic_slice_in_dim(all_counts, offset, per_turn, 0).reshape(
            8, TILE_ROW, TILE, TILE
        )
        target_part = lax.dynamic_slice_in_dim(target_blocks, iteration * 8, 8, 1)
        pieces = jnp.einsum(
            "fbt,bjst->fbjs", target_part, counts, preferred_element_type=jnp.float32
        )
        pieces = pieces.reshape(breadth, per_turn, TILE)
        return running.at[:, chosen, :].add(pieces)

    running = jnp.zeros((breadth, source_blocks, TILE), jnp.float32)
    return lax.fori_loop(0, block_count // 8, spread_advance, running).reshape(
        breadth, source_total
    )


def shards(
    src_feat,
    rel_w_in,
    rel_w_out,
    tile_source,
    tile_edges,
    tile_count,
    target_feat,
    norm_gain,
    tgt_w_in,
    tgt_w_out,
    out_grad,
):
    own_rows = src_feat[0]
    in_slice = rel_w_in[0]
    out_slice = rel_w_out[0]
    source_ids = tile_source[0]
    edge_codes = tile_edges[0]
    live_counts = tile_count[0]
    in_full, out_full = (
        lax.all_gather(in_slice, "dev", axis=0, tiled=True),
        lax.all_gather(out_slice, "dev", axis=0, tiled=True),
    )
    hidden_pre = jnp.dot(own_rows, in_full, preferred_element_type=jnp.float32)
    hidden = jax.nn.silu(hidden_pre).astype(jnp.bfloat16)
    mixed_cols = lax.dot_general(
        out_full, hidden, (((0,), (1,)), ((), ())), preferred_element_type=jnp.float32
    )
    mixed_cols = mixed_cols.astype(jnp.bfloat16)
    all_counts = tile_counts(edge_codes, live_counts)
    by_feature = lax.all_to_all(mixed_cols, "dev", split_axis=0, concat_axis=1, tiled=True)
    partial_value = aggregate(by_feature, source_ids, all_counts)
    source_total = by_feature.shape[1]
    gain_column = norm_gain[:, None]
    summed = lax.psum(partial_value, "rel")
    agg_cols = lax.all_to_all(summed, "dev", split_axis=1, concat_axis=0, tiled=True)
    inverse_norm = lax.rsqrt(jnp.mean(agg_cols * agg_cols, axis=0, keepdims=True) + eps_norm)
    normed = (agg_cols * inverse_norm * gain_column).astype(jnp.bfloat16)
    target_pre = lax.dot_general(
        normed, tgt_w_in, (((0,), (0,)), ((), ())), preferred_element_type=jnp.float32
    )
    target_hidden = jax.nn.silu(target_pre).astype(jnp.bfloat16)
    update = lax.psum_scatter(
        jnp.dot(target_hidden, tgt_w_out, preferred_element_type=jnp.float32),
        "rel",
        scatter_dimension=0,
        tiled=True,
    )
    updated = (target_feat.astype(jnp.float32) + update).astype(jnp.bfloat16)
    grad_hidden_t = lax.dot_general(
        lax.all_gather(out_grad, "rel", axis=0, tiled=True),
        tgt_w_out,
        (((1,), (1,)), ((), ())),
        preferred_element_type=jnp.float32,
    )
    grad_pre_t = (grad_hidden_t * silu_slope(target_pre)).astype(jnp.bfloat16)
    grad_normed = lax.dot_general(
        tgt_w_in, grad_pre_t, (((1,), (1,)), ((), ())), preferred_element_type=jnp.float32
    )
    grad_total = lax.psum(grad_normed, "rel")
    scaled = grad_total * gain_column
    mean_term = jnp.mean(agg_cols * scaled, axis=0, keepdims=True)
    grad_agg = (
        inverse_norm * (scaled - agg_cols * inverse_norm * inverse_norm * mean_term)
    ).astype(jnp.bfloat16)
    grad_targets = lax.all_to_all(grad_agg, "dev", split_axis=0, concat_axis=1, tiled=True)
    grad_mixed = spread(grad_targets, source_ids, all_counts, source_total).astype(jnp.bfloat16)
    grad_cols = lax.all_to_all(grad_mixed, "dev", split_axis=1, concat_axis=0, tiled=True)
    grad_hidden = lax.dot_general(
        grad_cols, out_full, (((0,), (1,)), ((), ())), preferred_element_type=jnp.float32
    )
    grad_pre = (grad_hidden * silu_slope(hidden_pre)).astype(jnp.bfloat16)
    grad_source = lax.dot_general(
        grad_pre, in_full, (((1,), (1,)), ((), ())), preferred_element_type=jnp.float32
    )
    return (updated, grad_source.astype(jnp.bfloat16)[None])


def solution(mesh):
    placed = (
        P("rel", "dev", None),
        P("rel", "dev", None),
        P("rel", "dev", None),
        P("rel", None),
        P("rel", None, None),
        P("rel", None),
        P(("dev", "rel"), None),
        P(),
        P(None, "rel"),
        P("rel", None),
        P(("dev", "rel"), None),
    )
    return jax.shard_map(
        shards,
        mesh=mesh,
        in_specs=placed,
        out_specs=(P(("dev", "rel"), None), P("rel", "dev", None)),
        check_vma=False,
    )
```

profile of v0, /device:TPU:0, one launch (start us, length us, event | category | flops | bytes accessed | tf_op | source)
XLA Modules:
  0.0 238.4 jit_solution(3827726353383810488)
XLA Ops:
  9.2 1.3 reduce.4
  12.0 28.4 %all-gather.5.cloned.1.call-done = bf16[1,1024,1024]{2,1,0:T(8,128)(2,1)} async-done(((bf16[1,128,1024]{2,1,0:T(8,128)(2,1)}), bf16[1,1024,1024]{2,1,0:T(8,128)(2,1)}) %all-gather.5.cloned.1.call-update) | async-done | bytes 2097168 | tf_op jit(solution)/shard_map/all_gather | solution.py:98
  40.4 2.5 %fusion.6 = f32[256,1024]{1,0:T(8,128)S(1)} fusion(bf16[1,1024,1024]{2,1,0:T(8,128)(2,1)} %all-gather.5.cloned.1.call-done, bf16[1,256,1024]{2,1,0:T(8,128)(2,1)} %param.11), kind=kOutput, calls=%fused_computation.8 | convolution fusion | flops 536870912 | bytes 3670016 | tf_op jit(solution)/shard_map/dot_general | solution.py:101
  42.9 27.2 %all-gather.7.cloned.1.call-done = bf16[1,1024,1024]{2,1,0:T(8,128)(2,1)} async-done(((bf16[1,128,1024]{2,1,0:T(8,128)(2,1)}), bf16[1,1024,1024]{2,1,0:T(8,128)(2,1)}) %all-gather.7.cloned.1.call-update) | async-done | bytes 2097168 | tf_op jit(solution)/shard_map/all_gather | solution.py:99
  70.1 2.3 fusion.26
  73.4 3.5 %all-to-all-start = ((bf16[8,128,256]{1,2,0:T(8,128)(2,1)}), bf16[8,128,256]{1,2,0:T(8,128)(2,1)S(1)}, u32[]{:S(2)}, u32[]{:S(2)}) async-start(bf16[8,128,256]{1,2,0:T(8,128)(2,1)} %bitcast.105), calls=%async_computation | async-start | bytes 1048576 | tf_op jit(solution)/shard_map/all_to_all | solution.py:108
  77.0 2.9 %fusion.11 = bf16[32,128,128]{2,1,0:T(8,128)(2,1)} fusion(s32[32,128]{1,0:T(8,128)S(1)} %get-tuple-element.27, s32[32,128]{1,0:T(8,128)S(1)} %get-tuple-element.26, pred[32,128]{1,0:T(8,128)(4,1)S(1)} %iota_compare_fusion.5), kind=kOutput, calls=%fused_computation.14 | convolution fusion | flops 136314880 | bytes 1085440 | tf_op jit(solution)/shard_map/kes,ket->kst/dot_general | solution.py:25
  79.9 6.6 %all-to-all-done = bf16[8,128,256]{1,2,0:T(8,128)(2,1)S(1)} async-done(((bf16[8,128,256]{1,2,0:T(8,128)(2,1)}), bf16[8,128,256]{1,2,0:T(8,128)(2,1)S(1)}, u32[]{:S(2)}, u32[]{:S(2)}) %all-to-all-start) | async-done | bytes 524320 | tf_op jit(solution)/shard_map/all_to_all | solution.py:108
  87.6 2.6 %convolution_bitcast_fusion = f32[128,8,128]{0,2,1:T(8,128)} fusion(bf16[8,4,128,128]{3,2,1,0:T(8,128)(2,1)} %bitcast.113, bf16[128,8,4,128]{3,0,2,1:T(8,128)(2,1)S(1)} %bitcast.112, pred[8,4]{1,0:T(8,128)(4,1)S(1)} %compare_and_fusion), kind=kOutput, calls=%fused_computation.19 | convolution fusion | flops 134742016 | bytes 2621472 | tf_op jit(solution)/shard_map/while/body/eval_jaxpr/fbjs,bjst->fbt/dot_general | solution.py:43
  90.2 37.8 %all-reduce.3.cloned.1.call-done = f32[128,8,128]{0,2,1:T(8,128)} async-done(((f32[128,8,128]{0,2,1:T(8,128)}), f32[128,8,128]{0,2,1:T(8,128)}) %all-reduce.3.cloned.1.call-update) | async-done | bytes 524304 | tf_op jit(solution)/shard_map/psum | solution.py:112
  128.0 3.6 %all-to-all-start.1 = ((f32[128,8,128]{0,2,1:T(8,128)}), f32[128,8,128]{0,2,1:T(8,128)S(1)}, u32[]{:S(2)}, u32[]{:S(2)}) async-start(f32[128,8,128]{0,2,1:T(8,128)} %all-reduce.3.cloned.1.call-done), calls=%async_computation.1 | async-start | bytes 1048576 | tf_op jit(solution)/shard_map/all_to_all | solution.py:113
  131.8 14.0 %all_gather.11 = bf16[128,1024]{1,0:T(8,128)(2,1)S(1)} all-gather(bf16[32,1024]{1,0:T(8,128)(2,1)S(1)} %copy-done.4), channel_id=1, replica_groups=mesh['rel'=4,'dev'=8] {'rel'}, dimensions={0}, use_global_device_ids=true | all-gather | bytes 327680 | tf_op jit(solution)/shard_map/all_gather | solution.py:128
  146.7 1.6 convolution_bitcast_fusion.1
  149.5 37.8 %all-reduce.5.cloned.1.call-done = f32[1024,128]{0,1:T(8,128)} async-done(((f32[1024,128]{0,1:T(8,128)}), f32[1024,128]{0,1:T(8,128)}) %all-reduce.5.cloned.1.call-update) | async-done | bytes 524304 | tf_op jit(solution)/shard_map/psum | solution.py:137
  190.0 10.3 %all_to_all.67 = bf16[8,128,128]{2,1,0:T(8,128)(2,1)S(1)} all-to-all(bf16[8,128,128]{2,1,0:T(8,128)(2,1)S(1)} %bitcast.115), channel_id=1, replica_groups=mesh['rel'=4,'dev'=8] {'dev'}, dimensions={0} | all-to-all | bytes 524288 | tf_op jit(solution)/shard_map/all_to_all | solution.py:143
  200.3 1.7 fusion.45
  202.0 1.8 copy.23
  203.9 4.7 %scatter_fusion = f32[128,16,128]{2,0,1:T(8,128)S(1)} fusion(f32[128,16,128]{2,0,1:T(8,128)S(1)} %broadcast_in_dim.30, s32[32]{0:T(128)S(1)} %fusion.59, f32[32,128,128]{2,1,0:T(8,128)} %bitcast.106), kind=kCustom, calls=%fused_computation.1 | custom fusion | flops 524288 | bytes 6291584 | tf_op jit(solution)/shard_map/while/body/eval_jaxpr/scatter-add | solution.py:70
  209.5 2.2 copy.24
  211.7 4.1 %all-to-all-start.3 = ((bf16[128,8,256]{0,2,1:T(8,128)(2,1)}), bf16[128,8,256]{0,2,1:T(8,128)(2,1)}, u32[]{:S(2)}, u32[]{:S(2)}) async-start(bf16[128,8,256]{0,2,1:T(8,128)(2,1)} %bitcast.110), calls=%async_computation.4 | async-start | bytes 1048576 | tf_op jit(solution)/shard_map/all_to_all | solution.py:145
  215.9 1.5 add_convert_fusion
  217.4 8.1 %all-to-all-done.3 = bf16[128,8,256]{0,2,1:T(8,128)(2,1)} async-done(((bf16[128,8,256]{0,2,1:T(8,128)(2,1)}), bf16[128,8,256]{0,2,1:T(8,128)(2,1)}, u32[]{:S(2)}, u32[]{:S(2)}) %all-to-all-start.3) | async-done | bytes 524320 | tf_op jit(solution)/shard_map/all_to_all | solution.py:145
  225.6 2.1 copy.25
  227.6 4.2 %fusion.29 = bf16[1,256,1024]{2,1,0:T(8,128)(2,1)} fusion(bf16[1,1024,1024]{2,1,0:T(8,128)(2,1)S(1)} %copy-done.1, bf16[1024,256]{1,0:T(8,128)(2,1)} %bitcast.116, bf16[1,1024,1024]{2,1,0:T(8,128)(2,1)} %all-gather.7.cloned.1.call-done, f32[256,1024]{1,0:T(8,128)} %copy-done.2), kind=kOutput, calls=%fused_computation.21 | convolution fusion | flops 1076363264 | bytes 6291456 | tf_op jit(solution)/shard_map/dot_general | solution.py:150
  (50 shorter events, 11.2 us)
Async XLA Ops:
  7.2 139.5 %copy-start = (bf16[512,1024]{1,0:T(8,128)(2,1)S(1)}, bf16[512,1024]{1,0:T(8,128)(2,1)}, u32[]{:S(2)}) copy-start(bf16[512,1024]{1,0:T(8,128)(2,1)} %param.20) | copy-start | bytes 3145732
  7.2 33.2 %all-gather.5.cloned.1.call-start = ((), (), s32[]{:S(2)}) async-start(), calls=%async_computation.8 | async-start | bytes 2359296 | tf_op jit(solution)/shard_map/all_gather | solution.py:98
  7.9 62.2 %all-gather.7.cloned.1.call-start = ((), (), s32[]{:S(2)}) async-start(), calls=%async_computation.9 | async-start | bytes 2359296 | tf_op jit(solution)/shard_map/all_gather | solution.py:99
  42.9 29.6 %copy-start.2 = (f32[256,1024]{1,0:T(8,128)}, f32[256,1024]{1,0:T(8,128)S(1)}, u32[]{:S(2)}) copy-start(f32[256,1024]{1,0:T(8,128)S(1)} %fusion.6) | copy-start | bytes 3145732
  72.5 4.5 %copy-start.7 = (s32[1,32]{1,0:T(1,128)S(1)}, s32[1,32]{1,0:T(1,128)}, u32[]{:S(2)}) copy-start(s32[1,32]{1,0:T(1,128)} %param.16) | copy-start | bytes 388
  73.4 13.2 %all-to-all-start = ((bf16[8,128,256]{1,2,0:T(8,128)(2,1)}), bf16[8,128,256]{1,2,0:T(8,128)(2,1)S(1)}, u32[]{:S(2)}, u32[]{:S(2)}) async-start(bf16[8,128,256]{1,2,0:T(8,128)(2,1)} %bitcast.105), calls=%async_computation | async-start | bytes 1048576 | tf_op jit(solution)/shard_map/all_to_all | solution.py:108
  76.9 51.2 %all-reduce.3.cloned.1.call-start = ((), (), s32[]{:S(2)}) async-start(), calls=%async_computation.5 | async-start | bytes 1048576 | tf_op jit(solution)/shard_map/psum | solution.py:112
  87.5 44.2 %copy-start.4 = (bf16[32,1024]{1,0:T(8,128)(2,1)S(1)}, bf16[32,1024]{1,0:T(8,128)(2,1)}, u32[]{:S(2)}) copy-start(bf16[32,1024]{1,0:T(8,128)(2,1)} %param.21) | copy-start | bytes 196612
  90.2 56.1 %copy-start.3 = (bf16[1024,512]{1,0:T(8,128)(2,1)S(1)}, bf16[1024,512]{1,0:T(8,128)(2,1)}, u32[]{:S(2)}) copy-start(bf16[1024,512]{1,0:T(8,128)(2,1)} %param.19) | copy-start | bytes 3145732
  90.2 56.1 %copy-start.6 = (f32[1024]{0:T(1024)S(1)}, f32[1024]{0:T(1024)}, u32[]{:S(2)}) copy-start(f32[1024]{0:T(1024)} %param.18) | copy-start | bytes 12292
  128.0 17.7 %all-to-all-start.1 = ((f32[128,8,128]{0,2,1:T(8,128)}), f32[128,8,128]{0,2,1:T(8,128)S(1)}, u32[]{:S(2)}, u32[]{:S(2)}) async-start(f32[128,8,128]{0,2,1:T(8,128)} %all-reduce.3.cloned.1.call-done), calls=%async_computation.1 | async-start | bytes 1048576 | tf_op jit(solution)/shard_map/all_to_all | solution.py:113
  131.7 55.7 %all-reduce.5.cloned.1.call-start = ((), (), s32[]{:S(2)}) async-start(), calls=%async_computation.7 | async-start | bytes 1048576 | tf_op jit(solution)/shard_map/psum | solution.py:137
  148.3 67.5 %reduce-scatter.2.cloned.1.call-start = ((), (), s32[]{:S(2)}) async-start(), calls=%async_computation.6 | async-start | bytes 655360 | tf_op jit(solution)/shard_map/reduce_scatter | solution.py:120
  208.6 7.3 %copy-start.5 = (bf16[32,1024]{1,0:T(8,128)(2,1)S(1)}, bf16[32,1024]{1,0:T(8,128)(2,1)}, u32[]{:S(2)}) copy-start(bf16[32,1024]{1,0:T(8,128)(2,1)} %param.17) | copy-start | bytes 196612
  209.5 18.1 %copy-start.1 = (bf16[1,1024,1024]{2,1,0:T(8,128)(2,1)S(1)}, bf16[1,1024,1024]{2,1,0:T(8,128)(2,1)}, u32[]{:S(2)}) copy-start(bf16[1,1024,1024]{2,1,0:T(8,128)(2,1)} %all-gather.5.cloned.1.call-done) | copy-start | bytes 6291460
  211.7 13.9 %all-to-all-start.3 = ((bf16[128,8,256]{0,2,1:T(8,128)(2,1)}), bf16[128,8,256]{0,2,1:T(8,128)(2,1)}, u32[]{:S(2)}, u32[]{:S(2)}) async-start(bf16[128,8,256]{0,2,1:T(8,128)(2,1)} %bitcast.110), calls=%async_computation.4 | async-start | bytes 1048576 | tf_op jit(solution)/shard_map/all_to_all | solution.py:145
Sparse Core Ops, SparseCore 0:
  9.9 30.4 all-gather.4
  42.3 27.7 all-gather.6
  90.3 37.6 all-reduce.2
  148.5 38.8 all-reduce.4
  190.1 21.6 reduce-scatter.1
where the time goes:
time: 239 us; the launch traced here: 238 us
  waiting for transfers between devices  147 us (62%)
  blocking collectives  24.3 us (10%)
  matrix products  19.3 us (8%)
  between operations  14 us (6%)
  other arithmetic  12.4 us (5%)
  starting transfers between devices  11.5 us (5%)
  local copies, waits for them, and re-layouts  9.34 us (4%)
    psum x1, waiting for transfers between devices, shards(): grad_total = lax.psum(grad_normed, 'rel')  37.8 us
    psum x1, waiting for transfers between devices, shards(): summed = lax.psum(partial_value, 'rel')  37.8 us
    all_gather x1, waiting for transfers between devices, shards(): lax.all_gather(in_slice, 'dev', axis=0, tiled=True)  28.4 us
    all_gather x1, waiting for transfers between devices, shards(): lax.all_gather(out_slice, 'dev', axis=0, tiled=True)  27.2 us
    all_gather x1, blocking collectives, shards(): lax.all_gather(out_grad, 'rel', axis=0, tiled=True)  14 us
    all_to_all x1, blocking collectives, shards(): lax.all_to_all(grad_agg, 'dev', split_axis=0, concat_axis=1, tiled=True)  10.3 us
    all_to_all x1, waiting for transfers between devices, shards(): lax.all_to_all(grad_mixed, 'dev', split_axis=1, concat_axis=0, tiled=True)  8.14 us
    all_to_all x1, waiting for transfers between devices, shards(): lax.all_to_all(mixed_cols, 'dev', split_axis=0, concat_axis=1, tiled=True)  6.58 us
  transfers between devices with their start and end apart: 8, of which 6 were waited for; matrix products, arithmetic and copies ran while one was open for 11% of the time, Pallas kernels for 0%

commit v1 on v0

v1 whole, which is shorter than its diff:
```python
import jax
import jax.numpy as jnp
from jax import lax
from jax.sharding import PartitionSpec as P

TILE = 128
TILE_ROW = 4


eps_norm = 1e-06


def silu_slope(values):
    sigma = jax.nn.sigmoid(values)
    return sigma * (1.0 + values * (1.0 - sigma))


def dot(a, b, ca=1, cb=0):
    return lax.dot_general(a, b, (((ca,), (cb,)), ((), ())), preferred_element_type=jnp.float32)


def swap(value, axis, size, mask):
    return lax.ppermute(value, axis, [(i, i ^ mask) for i in range(size)])


def own_counts(edge_codes, live_counts, source_ids, me, turn, own_rows, order):
    blocks = source_ids.shape[0] // TILE_ROW
    slots = edge_codes.shape[1]
    live = lax.broadcasted_iota(jnp.int32, edge_codes.shape, 1) < live_counts[:, None]
    source = source_ids[:, None] * TILE + edge_codes % TILE - me * own_rows
    source = jnp.where(live, source, -1)
    target = (edge_codes // TILE) ^ turn
    picked = jnp.asarray(order, jnp.int32) ^ me
    source = source.reshape(blocks, TILE_ROW * slots)[picked]
    target = target.reshape(blocks, TILE_ROW * slots)[picked]
    source_at = lax.broadcasted_iota(jnp.int32, (1, 1, own_rows), 2)
    target_at = lax.broadcasted_iota(jnp.int32, (1, 1, TILE), 2)
    source_hot = (source[:, :, None] == source_at).astype(jnp.bfloat16)
    target_hot = (target[:, :, None] == target_at).astype(jnp.bfloat16)
    counts = jnp.einsum("bet,bes->bts", target_hot, source_hot, preferred_element_type=jnp.float32)
    return counts.astype(jnp.bfloat16)


def make_shards(rels, devs):
    pairs = devs // 2
    evens = [2 * k for k in range(pairs)]
    odds = [2 * k + 1 for k in range(pairs)]

    def gather_dev(value):
        near = [value] + [swap(value, "dev", devs, 2 * k) for k in range(1, pairs)]
        near = jnp.concatenate(near, 0)
        return near, swap(near, "dev", devs, 1)

    def gather_rel(value):
        return jnp.concatenate([value] + [swap(value, "rel", rels, q) for q in range(1, rels)], 0)

    def reduce_rel(value):
        rows = value.shape[0] // rels
        total = value[:rows]
        for q in range(1, rels):
            piece = value[q * rows : (q + 1) * rows].astype(jnp.bfloat16)
            total = total + swap(piece, "rel", rels, q).astype(jnp.float32)
        return total

    def shards(
        src_feat,
        rel_w_in,
        rel_w_out,
        tile_source,
        tile_edges,
        tile_count,
        target_feat,
        norm_gain,
        tgt_w_in,
        tgt_w_out,
        out_grad,
    ):
        me = lax.axis_index("dev")
        rel = lax.axis_index("rel")
        own_rows = src_feat[0]
        rows = own_rows.shape[0]
        features = own_rows.shape[1]
        shard = rel_w_in.shape[1]
        gain = norm_gain[None, :]
        order = jnp.asarray(evens + odds, jnp.int32) ^ me

        in_near, in_far = gather_dev(rel_w_in[0])
        columns = own_rows.reshape(rows, devs, shard)[:, order].reshape(rows, 2, -1)
        hidden_pre = dot(columns[:, 0], in_near) + dot(columns[:, 1], in_far)
        hidden = jax.nn.silu(hidden_pre).astype(jnp.bfloat16)
        out_own, _ = lax.optimization_barrier((rel_w_out[0], in_near))
        out_near, out_far = gather_dev(out_own)

        def natural(near, far):
            both = jnp.concatenate([near, far], 0).reshape(devs, shard, -1)
            place = jnp.asarray([i // 2 + (i % 2) * pairs for i in range(devs)], jnp.int32)
            at = place[jnp.arange(devs, dtype=jnp.int32) ^ me]
            return both[at].reshape(devs * shard, -1)

        in_full = natural(in_near, in_far)
        out_full = natural(out_near, out_far)

        hidden_grad = dot(gather_rel(out_grad), tgt_w_out, 1, 1)

        sub = TILE // rels
        counts = own_counts(
            tile_edges[0], tile_count[0], tile_source[0], me, rel * sub, rows, evens + odds
        )
        counts = counts.reshape(2, pairs * TILE, rows)
        far = swap(dot(counts[1], hidden).astype(jnp.bfloat16), "dev", devs, 1)
        near = dot(counts[0], hidden) + far.astype(jnp.float32)
        total = near[:TILE]
        for k in range(1, pairs):
            piece = near[k * TILE : (k + 1) * TILE].astype(jnp.bfloat16)
            total = total + swap(piece, "dev", devs, 2 * k).astype(jnp.float32)
        agg = reduce_rel(dot(total.astype(jnp.bfloat16), out_full))

        inverse_norm = lax.rsqrt(jnp.mean(agg * agg, axis=1, keepdims=True) + eps_norm)
        normed = gather_rel((agg * inverse_norm * gain).astype(jnp.bfloat16))
        target_pre = dot(normed, tgt_w_in)
        grad_pre_t = (hidden_grad * silu_slope(target_pre)).astype(jnp.bfloat16)
        grad_normed = reduce_rel(dot(grad_pre_t, tgt_w_in, 1, 1))
        target_hidden = jax.nn.silu(target_pre).astype(jnp.bfloat16)
        scaled = grad_normed * gain
        mean_term = jnp.mean(agg * scaled, axis=1, keepdims=True)
        grad_agg = inverse_norm * (scaled - agg * inverse_norm * inverse_norm * mean_term)
        grad_agg = gather_rel(grad_agg.astype(jnp.bfloat16))
        target_hidden, grad_agg = lax.optimization_barrier((target_hidden, grad_agg))
        update = reduce_rel(dot(target_hidden, tgt_w_out))
        updated = (target_feat.astype(jnp.float32) + update).astype(jnp.bfloat16)

        back_near, back_far = gather_dev(dot(grad_agg, out_full, 1, 1).astype(jnp.bfloat16))
        grad_hidden = dot(counts[0], back_near, 0, 0) + dot(counts[1], back_far, 0, 0)
        grad_pre = (grad_hidden * silu_slope(hidden_pre)).astype(jnp.bfloat16)
        grad_source = dot(grad_pre, in_full, 1, 1)
        return (updated, grad_source.astype(jnp.bfloat16)[None])

    return shards


def solution(mesh):
    placed = (
        P("rel", "dev", None),
        P("rel", "dev", None),
        P("rel", "dev", None),
        P("rel", None),
        P("rel", None, None),
        P("rel", None),
        P(("dev", "rel"), None),
        P(),
        P(None, "rel"),
        P("rel", None),
        P(("dev", "rel"), None),
    )
    return jax.shard_map(
        make_shards(mesh.shape["rel"], mesh.shape["dev"]),
        mesh=mesh,
        in_specs=placed,
        out_specs=(P(("dev", "rel"), None), P("rel", "dev", None)),
        check_vma=False,
    )
```

time: 239 us -> 147 us (0.62)
  waiting for transfers between devices: 147 us -> 58.3 us
  starting transfers between devices: 11.5 us -> 42 us
  blocking collectives: 24.3 us -> 0 us
  between operations: 14 us -> 1.2 us
  local copies, waits for them, and re-layouts: 9.34 us -> 15.7 us
  other arithmetic: 12.4 us -> 8.69 us
    psum x2 -> x0, waiting for transfers between devices: 75.7 us -> none  [the longest x1 37.8 us: shards(): grad_total = lax.psum(grad_normed, 'rel')]
    ppermute x0 -> x34, waiting for transfers between devices: none -> 58.3 us  [swap(): return lax.ppermute(value, axis, [(i, i ^ mask) for i in range(size)])]
    all_gather x2 -> x0, waiting for transfers between devices: 55.6 us -> none  [the longest x1 28.4 us: shards(): lax.all_gather(in_slice, 'dev', axis=0, tiled=True)]
    ppermute x0 -> x34, starting transfers between devices: none -> 42 us  [swap(): return lax.ppermute(value, axis, [(i, i ^ mask) for i in range(size)])]
    all_to_all x3 -> x0, waiting for transfers between devices: 14.7 us -> none  [the longest x1 8.14 us: shards(): lax.all_to_all(grad_mixed, 'dev', split_axis=1, concat_axis=0, tiled=True)]
    all_gather x1 -> x0, blocking collectives: 14 us -> none  [shards(): lax.all_gather(out_grad, 'rel', axis=0, tiled=True)]
    all_to_all x3 -> x0, starting transfers between devices: 11.3 us -> none  [the longest x1 4.14 us: shards(): lax.all_to_all(grad_mixed, 'dev', split_axis=1, concat_axis=0, tiled=True)]
    all_to_all x1 -> x0, blocking collectives: 10.3 us -> none  [shards(): lax.all_to_all(grad_agg, 'dev', split_axis=0, concat_axis=1, tiled=True)]
  transfers between devices with their start and end apart: 8 -> 34, of which waited for: 6 -> 22; matrix products, arithmetic and copies ran while one was open for 11% -> 13% of each run, Pallas kernels for 0% -> 0%
where the time goes in v1:
time: 147 us; the launch traced here: 146 us
  waiting for transfers between devices  58.3 us (40%)
  starting transfers between devices  42 us (29%)
  matrix products  20.4 us (14%)
  local copies, waits for them, and re-layouts  15.7 us (11%)
  other arithmetic  8.69 us (6%)
    ppermute x34, waiting for transfers between devices, swap(): return lax.ppermute(value, axis, [(i, i ^ mask) for i in range(size)])  58.3 us
    ppermute x34, starting transfers between devices, swap(): return lax.ppermute(value, axis, [(i, i ^ mask) for i in range(size)])  42 us
    dot_general x11, matrix products, dot(): lax.dot_general(a, b, (((ca,), (cb,)), ((), ())), preferred_element_type=...  19.1 us
    unnamed x86, local copies, waits for them, and re-layouts  4.78 us
    gather x2, local copies, waits for them, and re-layouts, natural(): return both[at].reshape(devs * shard, -1)  4.27 us
    concatenate x3, other arithmetic, gather_dev(): near = jnp.concatenate(near, 0)  3.25 us
  transfers between devices with their start and end apart: 34, of which 22 were waited for; matrix products, arithmetic and copies ran while one was open for 13% of the time, Pallas kernels for 0%

profile of v1, /device:TPU:0, one launch (start us, length us, event | category | flops | bytes accessed | tf_op | source)
XLA Modules:
  0.0 146.3 jit_solution(12399605664047181895)
XLA Ops:
  0.7 3.0 %collective-permute-start = (bf16[128,1024]{1,0:T(8,128)(2,1)}, bf16[128,1024]{1,0:T(8,128)(2,1)S(1)}, u32[]{:S(2)}, u32[]{:S(2)}) collective-permute-start(bf16[128,1024]{1,0:T(8,128)(2,1)} %bitcast.67), channel_id=1, source_target_pairs={{0,2},{1,3},{2,0},{3,1},{4,6},{5,7},{6,4},{7,5},{8,10},{9,11},{10,... | collective-permute-start | bytes 786440 | tf_op jit(solution)/shard_map/ppermute | solution.py:23
  5.9 5.2 %collective-permute-done = bf16[128,1024]{1,0:T(8,128)(2,1)S(1)} collective-permute-done((bf16[128,1024]{1,0:T(8,128)(2,1)}, bf16[128,1024]{1,0:T(8,128)(2,1)S(1)}, u32[]{:S(2)}, u32[]{:S(2)}) %collective-permute-start) | collective-permute-done | bytes 262176 | tf_op jit(solution)/shard_map/ppermute | solution.py:23
  11.1 6.2 %collective-permute-done.1 = bf16[128,1024]{1,0:T(8,128)(2,1)S(1)} collective-permute-done((bf16[128,1024]{1,0:T(8,128)(2,1)}, bf16[128,1024]{1,0:T(8,128)(2,1)S(1)}, u32[]{:S(2)}, u32[]{:S(2)}) %collective-permute-start.1) | collective-permute-done | bytes 262176 | tf_op jit(solution)/shard_map/ppermute | solution.py:23
  18.0 2.0 %pad_maximum_fusion = bf16[512,1024]{1,0:T(8,128)(2,1)} fusion(bf16[128,1024]{1,0:T(8,128)(2,1)S(1)} %collective-permute-done.2, bf16[128,1024]{1,0:T(8,128)(2,1)S(1)} %collective-permute-done.1, bf16[128,1024]{1,0:T(8,128)(2,1)S(1)} %collective-permute-done, bf16[128,1024]{1,0:T(8,128)(2,1)} %bitcast.70), kind=kLoop, calls=%fused_computation.23 | loop fusion | flops 4194304 | bytes 2097152 | tf_op jit(solution)/shard_map/concatenate | solution.py:51
  34.9 5.7 %collective-permute-done.8 = bf16[128,1024]{1,0:T(8,128)(2,1)S(1)} collective-permute-done((bf16[128,1024]{1,0:T(8,128)(2,1)S(1)}, bf16[128,1024]{1,0:T(8,128)(2,1)S(1)}, u32[]{:S(2)}, u32[]{:S(2)}) %collective-permute-start.8) | collective-permute-done | bytes 262176 | tf_op jit(solution)/shard_map/ppermute | solution.py:23
  40.5 4.0 %collective-permute-done.9 = bf16[128,1024]{1,0:T(8,128)(2,1)S(1)} collective-permute-done((bf16[128,1024]{1,0:T(8,128)(2,1)S(1)}, bf16[128,1024]{1,0:T(8,128)(2,1)S(1)}, u32[]{:S(2)}, u32[]{:S(2)}) %collective-permute-start.9) | collective-permute-done | bytes 262176 | tf_op jit(solution)/shard_map/ppermute | solution.py:23
  54.2 2.3 %gather_fusion.4 = bf16[8,128,1024]{2,1,0:T(8,128)(2,1)S(1)} fusion(bf16[8,128,1024]{2,1,0:T(8,128)(2,1)} %bitcast.53, s32[1024]{0:T(1024)S(1)} %pad_clamp_fusion), kind=kCustom, calls=%fused_computation.4 | custom fusion | bytes 4194336 | tf_op jit(solution)/shard_map/gather | solution.py:98
  56.4 2.2 %collective-permute-done.5 = bf16[128,1024]{1,0:T(8,128)(2,1)} collective-permute-done((bf16[128,1024]{1,0:T(8,128)(2,1)}, bf16[128,1024]{1,0:T(8,128)(2,1)}, u32[]{:S(2)}, u32[]{:S(2)}) %collective-permute-start.5) | collective-permute-done | bytes 262176 | tf_op jit(solution)/shard_map/ppermute | solution.py:23
  58.7 5.7 %collective-permute-done.6 = bf16[128,1024]{1,0:T(8,128)(2,1)} collective-permute-done((bf16[128,1024]{1,0:T(8,128)(2,1)}, bf16[128,1024]{1,0:T(8,128)(2,1)}, u32[]{:S(2)}, u32[]{:S(2)}) %collective-permute-start.6) | collective-permute-done | bytes 262176 | tf_op jit(solution)/shard_map/ppermute | solution.py:23
  67.9 2.6 %collective-permute-start.13 = (bf16[32,1024]{1,0:T(8,128)(2,1)S(1)}, bf16[32,1024]{1,0:T(8,128)(2,1)S(1)}, u32[]{:S(2)}, u32[]{:S(2)}) collective-permute-start(bf16[32,1024]{1,0:T(8,128)(2,1)S(1)} %get-tuple-element.23), channel_id=1, source_target_pairs={{0,16},{8,24},{16,0},{24,8},{1,17},{9,25},{17,1},{25,9},{2,18},{10... | collective-permute-start | bytes 196616 | tf_op jit(solution)/shard_map/ppermute | solution.py:23
  70.7 4.0 %collective-permute-done.13 = bf16[32,1024]{1,0:T(8,128)(2,1)S(1)} collective-permute-done((bf16[32,1024]{1,0:T(8,128)(2,1)S(1)}, bf16[32,1024]{1,0:T(8,128)(2,1)S(1)}, u32[]{:S(2)}, u32[]{:S(2)}) %collective-permute-start.13) | collective-permute-done | bytes 65568 | tf_op jit(solution)/shard_map/ppermute | solution.py:23
  78.8 2.5 %collective-permute-start.17 = (bf16[32,1024]{1,0:T(8,128)(2,1)S(1)}, bf16[32,1024]{1,0:T(8,128)(2,1)S(1)}, u32[]{:S(2)}, u32[]{:S(2)}) collective-permute-start(bf16[32,1024]{1,0:T(8,128)(2,1)S(1)} %multiply_convert_fusion.3), channel_id=1, source_target_pairs={{0,24},{8,16},{16,8},{24,0},{1,25},{9,17},{17,9},{25,1},{2,26},{10... | collective-permute-start | bytes 196616 | tf_op jit(solution)/shard_map/ppermute | solution.py:23
  83.5 2.1 %collective-permute-start.20 = (bf16[32,1024]{1,0:T(8,128)(2,1)S(1)}, bf16[32,1024]{1,0:T(8,128)(2,1)S(1)}, u32[]{:S(2)}, u32[]{:S(2)}) collective-permute-start(bf16[32,1024]{1,0:T(8,128)(2,1)S(1)} %copy-done.30), channel_id=1, source_target_pairs={{0,24},{8,16},{16,8},{24,0},{1,25},{9,17},{17,9},{25,1},{2,26},{10... | collective-permute-start | bytes 196616 | tf_op jit(solution)/shard_map/ppermute | solution.py:23
  90.3 3.2 %fusion.74 = (bf16[128,1024]{1,0:T(8,128)(2,1)}, f32[128,1024]{1,0:T(8,128)}) fusion(bf16[1024,512]{1,0:T(8,128)(2,1)} %param.23, bf16[512,1024]{1,0:T(8,128)(2,1)S(1)} %copy-done, bf16[32,1024]{1,0:T(8,128)(2,1)} %copy-done.33, bf16[32,1024]{1,0:T(8,128)(2,1)} %copy-done.32, bf16[32,1024]{1,0:T(8,128)(2,1)} %copy-done.31, bf16[32,1024]{1,0:T(8,128)(2,1)} %param.25, ...), kind=kOutput, calls=%fused_computation.124 | convolution fusion | flops 270204928 | bytes 3407872 | tf_op jit(solution)/shard_map/dot_general | solution.py:19
  99.5 2.0 %collective-permute-done.22 = bf16[32,1024]{1,0:T(8,128)(2,1)S(1)} collective-permute-done((bf16[32,1024]{1,0:T(8,128)(2,1)S(1)}, bf16[32,1024]{1,0:T(8,128)(2,1)S(1)}, u32[]{:S(2)}, u32[]{:S(2)}) %collective-permute-start.22) | collective-permute-done | bytes 65568 | tf_op jit(solution)/shard_map/ppermute | solution.py:23
  105.5 2.4 %collective-permute-start.25 = (bf16[32,1024]{1,0:T(8,128)(2,1)S(1)}, bf16[32,1024]{1,0:T(8,128)(2,1)S(1)}, u32[]{:S(2)}, u32[]{:S(2)}) collective-permute-start(bf16[32,1024]{1,0:T(8,128)(2,1)S(1)} %multiply_convert_fusion.2), channel_id=1, source_target_pairs={{0,16},{8,24},{16,0},{24,8},{1,17},{9,25},{17,1},{25,9},{2,18},{10... | collective-permute-start | bytes 196616 | tf_op jit(solution)/shard_map/ppermute | solution.py:23
  107.8 2.0 %collective-permute-start.26 = (bf16[32,1024]{1,0:T(8,128)(2,1)S(1)}, bf16[32,1024]{1,0:T(8,128)(2,1)S(1)}, u32[]{:S(2)}, u32[]{:S(2)}) collective-permute-start(bf16[32,1024]{1,0:T(8,128)(2,1)S(1)} %multiply_convert_fusion.2), channel_id=1, source_target_pairs={{0,24},{8,16},{16,8},{24,0},{1,25},{9,17},{17,9},{25,1},{2,26},{10... | collective-permute-start | bytes 196616 | tf_op jit(solution)/shard_map/ppermute | solution.py:23
  110.7 3.2 %collective-permute-done.26 = bf16[32,1024]{1,0:T(8,128)(2,1)S(1)} collective-permute-done((bf16[32,1024]{1,0:T(8,128)(2,1)S(1)}, bf16[32,1024]{1,0:T(8,128)(2,1)S(1)}, u32[]{:S(2)}, u32[]{:S(2)}) %collective-permute-start.26) | collective-permute-done | bytes 65568 | tf_op jit(solution)/shard_map/ppermute | solution.py:23
  118.4 2.8 %collective-permute-done.30 = bf16[128,1024]{1,0:T(8,128)(2,1)S(1)} collective-permute-done((bf16[128,1024]{1,0:T(8,128)(2,1)S(1)}, bf16[128,1024]{1,0:T(8,128)(2,1)S(1)}, u32[]{:S(2)}, u32[]{:S(2)}) %collective-permute-start.30) | collective-permute-done | bytes 262176 | tf_op jit(solution)/shard_map/ppermute | solution.py:23
  121.2 4.5 %collective-permute-done.31 = bf16[128,1024]{1,0:T(8,128)(2,1)S(1)} collective-permute-done((bf16[128,1024]{1,0:T(8,128)(2,1)S(1)}, bf16[128,1024]{1,0:T(8,128)(2,1)S(1)}, u32[]{:S(2)}, u32[]{:S(2)}) %collective-permute-start.31) | collective-permute-done | bytes 262176 | tf_op jit(solution)/shard_map/ppermute | solution.py:23
  128.8 2.9 %collective-permute-start.28 = (bf16[32,1024]{1,0:T(8,128)(2,1)}, bf16[32,1024]{1,0:T(8,128)(2,1)}, u32[]{:S(2)}, u32[]{:S(2)}) collective-permute-start(bf16[32,1024]{1,0:T(8,128)(2,1)} %get-tuple-element.17), channel_id=1, source_target_pairs={{0,16},{8,24},{16,0},{24,8},{1,17},{9,25},{17,1},{25,9},{2,18},{10... | collective-permute-start | bytes 196616 | tf_op jit(solution)/shard_map/ppermute | solution.py:23
  133.2 2.0 %gather_fusion.5 = bf16[8,128,1024]{2,1,0:T(8,128)(2,1)} fusion(bf16[8,128,1024]{2,1,0:T(8,128)(2,1)S(1)} %bitcast.54, s32[1024]{0:T(1024)S(1)} %pad_clamp_fusion), kind=kCustom, calls=%fused_computation.5 | custom fusion | bytes 4194336 | tf_op jit(solution)/shard_map/gather | solution.py:98
  139.7 2.7 %fusion.78 = f32[256,1024]{1,0:T(8,128)} fusion(bf16[512,256]{1,0:T(8,128)(2,1)S(1)} %bitcast.61, bf16[512,1024]{1,0:T(8,128)(2,1)} %collective-permute-done.33), kind=kOutput, calls=%fused_computation.126 | convolution fusion | flops 268435456 | bytes 2359296 | tf_op jit(solution)/shard_map/dot_general | solution.py:19
  142.3 4.0 %fusion.5 = bf16[1,256,1024]{2,1,0:T(8,128)(2,1)} fusion(bf16[1024,1024]{1,0:T(8,128)(2,1)S(1)} %bitcast.55, f32[256,1024]{1,0:T(8,128)} %fusion.78, bf16[512,256]{1,0:T(8,128)(2,1)} %bitcast.73, f32[256,1024]{1,0:T(8,128)} %copy-done.36, bf16[128,1024]{1,0:T(8,128)(2,1)} %copy-done.24, bf16[128,1024]{1,0:T(8,128)(2,1)} %copy-done.23, ...), kind=kOutput, calls=%fused_computation.18 | convolution fusion | flops 812384256 | bytes 6029312 | tf_op jit(solution)/shard_map/dot_general | solution.py:19
  (182 shorter events, 66.0 us)
Async XLA Ops:
  0.7 10.4 %collective-permute-start = (bf16[128,1024]{1,0:T(8,128)(2,1)}, bf16[128,1024]{1,0:T(8,128)(2,1)S(1)}, u32[]{:S(2)}, u32[]{:S(2)}) collective-permute-start(bf16[128,1024]{1,0:T(8,128)(2,1)} %bitcast.67), channel_id=1, source_target_pairs={{0,2},{1,3},{2,0},{3,1},{4,6},{5,7},{6,4},{7,5},{8,10},{9,11},{10,... | collective-permute-start | bytes 786440 | tf_op jit(solution)/shard_map/ppermute | solution.py:23
  3.7 13.6 %collective-permute-start.1 = (bf16[128,1024]{1,0:T(8,128)(2,1)}, bf16[128,1024]{1,0:T(8,128)(2,1)S(1)}, u32[]{:S(2)}, u32[]{:S(2)}) collective-permute-start(bf16[128,1024]{1,0:T(8,128)(2,1)} %bitcast.68), channel_id=1, source_target_pairs={{0,4},{1,5},{2,6},{3,7},{4,0},{5,1},{6,2},{7,3},{8,12},{9,13},{10,... | collective-permute-start | bytes 786440 | tf_op jit(solution)/shard_map/ppermute | solution.py:23
  5.2 12.1 %collective-permute-start.2 = (bf16[128,1024]{1,0:T(8,128)(2,1)}, bf16[128,1024]{1,0:T(8,128)(2,1)S(1)}, u32[]{:S(2)}, u32[]{:S(2)}) collective-permute-start(bf16[128,1024]{1,0:T(8,128)(2,1)} %bitcast.69), channel_id=1, source_target_pairs={{0,6},{1,7},{2,4},{3,5},{4,2},{5,3},{6,0},{7,1},{8,14},{9,15},{10,... | collective-permute-start | bytes 786440 | tf_op jit(solution)/shard_map/ppermute | solution.py:23
  20.1 6.4 %collective-permute-start.3 = (bf16[512,1024]{1,0:T(8,128)(2,1)}, bf16[512,1024]{1,0:T(8,128)(2,1)S(1)}, u32[]{:S(2)}, u32[]{:S(2)}) collective-permute-start(bf16[512,1024]{1,0:T(8,128)(2,1)} %pad_maximum_fusion), channel_id=1, source_target_pairs={{0,1},{1,0},{2,3},{3,2},{4,5},{5,4},{6,7},{7,6},{8,9},{9,8},{10,11... | collective-permute-start | bytes 3145736 | tf_op jit(solution)/shard_map/ppermute | solution.py:23
  30.2 16.2 %collective-permute-start.4 = (bf16[512,1024]{1,0:T(8,128)(2,1)}, bf16[512,1024]{1,0:T(8,128)(2,1)S(1)}, u32[]{:S(2)}, u32[]{:S(2)}) collective-permute-start(bf16[512,1024]{1,0:T(8,128)(2,1)} %convolution_convert_fusion), channel_id=1, source_target_pairs={{0,1},{1,0},{2,3},{3,2},{4,5},{5,4},{6,7},{7,6},{8,9},{9,8},{10,11... | collective-permute-start | bytes 3145736 | tf_op jit(solution)/shard_map/ppermute | solution.py:23
  31.3 9.2 %collective-permute-start.8 = (bf16[128,1024]{1,0:T(8,128)(2,1)S(1)}, bf16[128,1024]{1,0:T(8,128)(2,1)S(1)}, u32[]{:S(2)}, u32[]{:S(2)}) collective-permute-start(bf16[128,1024]{1,0:T(8,128)(2,1)S(1)} %bitcast.62), channel_id=1, source_target_pairs={{0,2},{1,3},{2,0},{3,1},{4,6},{5,7},{6,4},{7,5},{8,10},{9,11},{10,... | collective-permute-start | bytes 786440 | tf_op jit(solution)/shard_map/ppermute | solution.py:23
  32.6 12.0 %collective-permute-start.9 = (bf16[128,1024]{1,0:T(8,128)(2,1)S(1)}, bf16[128,1024]{1,0:T(8,128)(2,1)S(1)}, u32[]{:S(2)}, u32[]{:S(2)}) collective-permute-start(bf16[128,1024]{1,0:T(8,128)(2,1)S(1)} %bitcast.63), channel_id=1, source_target_pairs={{0,4},{1,5},{2,6},{3,7},{4,0},{5,1},{6,2},{7,3},{8,12},{9,13},{10,... | collective-permute-start | bytes 786440 | tf_op jit(solution)/shard_map/ppermute | solution.py:23
  33.4 12.7 %collective-permute-start.10 = (bf16[128,1024]{1,0:T(8,128)(2,1)S(1)}, bf16[128,1024]{1,0:T(8,128)(2,1)S(1)}, u32[]{:S(2)}, u32[]{:S(2)}) collective-permute-start(bf16[128,1024]{1,0:T(8,128)(2,1)S(1)} %bitcast.64), channel_id=1, source_target_pairs={{0,6},{1,7},{2,4},{3,5},{4,2},{5,3},{6,0},{7,1},{8,14},{9,15},{10,... | collective-permute-start | bytes 786440 | tf_op jit(solution)/shard_map/ppermute | solution.py:23
  46.2 6.5 %collective-permute-start.11 = (bf16[512,1024]{1,0:T(8,128)(2,1)S(1)}, bf16[512,1024]{1,0:T(8,128)(2,1)S(1)}, u32[]{:S(2)}, u32[]{:S(2)}) collective-permute-start(bf16[512,1024]{1,0:T(8,128)(2,1)S(1)} %pad_maximum_fusion.1), channel_id=1, source_target_pairs={{0,1},{1,0},{2,3},{3,2},{4,5},{5,4},{6,7},{7,6},{8,9},{9,8},{10,11... | collective-permute-start | bytes 3145736 | tf_op jit(solution)/shard_map/ppermute | solution.py:23
  49.2 9.5 %collective-permute-start.5 = (bf16[128,1024]{1,0:T(8,128)(2,1)}, bf16[128,1024]{1,0:T(8,128)(2,1)}, u32[]{:S(2)}, u32[]{:S(2)}) collective-permute-start(bf16[128,1024]{1,0:T(8,128)(2,1)} %get-tuple-element.10), channel_id=1, source_target_pairs={{0,2},{1,3},{2,0},{3,1},{4,6},{5,7},{6,4},{7,5},{8,10},{9,11},{10,... | collective-permute-start | bytes 786440 | tf_op jit(solution)/shard_map/ppermute | solution.py:23
  50.0 14.4 %collective-permute-start.6 = (bf16[128,1024]{1,0:T(8,128)(2,1)}, bf16[128,1024]{1,0:T(8,128)(2,1)}, u32[]{:S(2)}, u32[]{:S(2)}) collective-permute-start(bf16[128,1024]{1,0:T(8,128)(2,1)} %get-tuple-element.12), channel_id=1, source_target_pairs={{0,4},{1,5},{2,6},{3,7},{4,0},{5,1},{6,2},{7,3},{8,12},{9,13},{10,... | collective-permute-start | bytes 786440 | tf_op jit(solution)/shard_map/ppermute | solution.py:23
  51.5 12.8 %collective-permute-start.7 = (bf16[128,1024]{1,0:T(8,128)(2,1)}, bf16[128,1024]{1,0:T(8,128)(2,1)}, u32[]{:S(2)}, u32[]{:S(2)}) collective-permute-start(bf16[128,1024]{1,0:T(8,128)(2,1)} %get-tuple-element.11), channel_id=1, source_target_pairs={{0,6},{1,7},{2,4},{3,5},{4,2},{5,3},{6,0},{7,1},{8,14},{9,15},{10,... | collective-permute-start | bytes 786440 | tf_op jit(solution)/shard_map/ppermute | solution.py:23
  67.9 6.8 %collective-permute-start.13 = (bf16[32,1024]{1,0:T(8,128)(2,1)S(1)}, bf16[32,1024]{1,0:T(8,128)(2,1)S(1)}, u32[]{:S(2)}, u32[]{:S(2)}) collective-permute-start(bf16[32,1024]{1,0:T(8,128)(2,1)S(1)} %get-tuple-element.23), channel_id=1, source_target_pairs={{0,16},{8,24},{16,0},{24,8},{1,17},{9,25},{17,1},{25,9},{2,18},{10... | collective-permute-start | bytes 196616 | tf_op jit(solution)/shard_map/ppermute | solution.py:23
  76.8 6.7 %collective-permute-start.15 = (bf16[32,1024]{1,0:T(8,128)(2,1)S(1)}, bf16[32,1024]{1,0:T(8,128)(2,1)S(1)}, u32[]{:S(2)}, u32[]{:S(2)}) collective-permute-start(bf16[32,1024]{1,0:T(8,128)(2,1)S(1)} %multiply_convert_fusion.3), channel_id=1, source_target_pairs={{0,8},{8,0},{16,24},{24,16},{1,9},{9,1},{17,25},{25,17},{2,10},{10... | collective-permute-start | bytes 196616 | tf_op jit(solution)/shard_map/ppermute | solution.py:23
  76.9 8.8 %collective-permute-start.16 = (bf16[32,1024]{1,0:T(8,128)(2,1)S(1)}, bf16[32,1024]{1,0:T(8,128)(2,1)S(1)}, u32[]{:S(2)}, u32[]{:S(2)}) collective-permute-start(bf16[32,1024]{1,0:T(8,128)(2,1)S(1)} %multiply_convert_fusion.3), channel_id=1, source_target_pairs={{0,16},{8,24},{16,0},{24,8},{1,17},{9,25},{17,1},{25,9},{2,18},{10... | collective-permute-start | bytes 196616 | tf_op jit(solution)/shard_map/ppermute | solution.py:23
  78.8 7.0 %collective-permute-start.17 = (bf16[32,1024]{1,0:T(8,128)(2,1)S(1)}, bf16[32,1024]{1,0:T(8,128)(2,1)S(1)}, u32[]{:S(2)}, u32[]{:S(2)}) collective-permute-start(bf16[32,1024]{1,0:T(8,128)(2,1)S(1)} %multiply_convert_fusion.3), channel_id=1, source_target_pairs={{0,24},{8,16},{16,8},{24,0},{1,25},{9,17},{17,9},{25,1},{2,26},{10... | collective-permute-start | bytes 196616 | tf_op jit(solution)/shard_map/ppermute | solution.py:23
  81.2 7.6 %collective-permute-start.19 = (bf16[32,1024]{1,0:T(8,128)(2,1)S(1)}, bf16[32,1024]{1,0:T(8,128)(2,1)S(1)}, u32[]{:S(2)}, u32[]{:S(2)}) collective-permute-start(bf16[32,1024]{1,0:T(8,128)(2,1)S(1)} %copy-done.30), channel_id=1, source_target_pairs={{0,16},{8,24},{16,0},{24,8},{1,17},{9,25},{17,1},{25,9},{2,18},{10... | collective-permute-start | bytes 196616 | tf_op jit(solution)/shard_map/ppermute | solution.py:23
  114.8 6.4 %collective-permute-start.30 = (bf16[128,1024]{1,0:T(8,128)(2,1)S(1)}, bf16[128,1024]{1,0:T(8,128)(2,1)S(1)}, u32[]{:S(2)}, u32[]{:S(2)}) collective-permute-start(bf16[128,1024]{1,0:T(8,128)(2,1)S(1)} %convolution_convert_fusion.2), channel_id=1, source_target_pairs={{0,2},{1,3},{2,0},{3,1},{4,6},{5,7},{6,4},{7,5},{8,10},{9,11},{10,... | collective-permute-start | bytes 786440 | tf_op jit(solution)/shard_map/ppermute | solution.py:23
  116.5 9.2 %collective-permute-start.31 = (bf16[128,1024]{1,0:T(8,128)(2,1)S(1)}, bf16[128,1024]{1,0:T(8,128)(2,1)S(1)}, u32[]{:S(2)}, u32[]{:S(2)}) collective-permute-start(bf16[128,1024]{1,0:T(8,128)(2,1)S(1)} %convolution_convert_fusion.2), channel_id=1, source_target_pairs={{0,4},{1,5},{2,6},{3,7},{4,0},{5,1},{6,2},{7,3},{8,12},{9,13},{10,... | collective-permute-start | bytes 786440 | tf_op jit(solution)/shard_map/ppermute | solution.py:23
  116.9 8.8 %collective-permute-start.32 = (bf16[128,1024]{1,0:T(8,128)(2,1)S(1)}, bf16[128,1024]{1,0:T(8,128)(2,1)S(1)}, u32[]{:S(2)}, u32[]{:S(2)}) collective-permute-start(bf16[128,1024]{1,0:T(8,128)(2,1)S(1)} %convolution_convert_fusion.2), channel_id=1, source_target_pairs={{0,6},{1,7},{2,4},{3,5},{4,2},{5,3},{6,0},{7,1},{8,14},{9,15},{10,... | collective-permute-start | bytes 786440 | tf_op jit(solution)/shard_map/ppermute | solution.py:23
  126.9 12.8 %collective-permute-start.33 = (bf16[512,1024]{1,0:T(8,128)(2,1)}, bf16[512,1024]{1,0:T(8,128)(2,1)}, u32[]{:S(2)}, u32[]{:S(2)}) collective-permute-start(bf16[512,1024]{1,0:T(8,128)(2,1)} %pad_maximum_fusion.2), channel_id=1, source_target_pairs={{0,1},{1,0},{2,3},{3,2},{4,5},{5,4},{6,7},{7,6},{8,9},{9,8},{10,11... | collective-permute-start | bytes 3145736 | tf_op jit(solution)/shard_map/ppermute | solution.py:23
  128.8 6.5 %collective-permute-start.27 = (bf16[32,1024]{1,0:T(8,128)(2,1)}, bf16[32,1024]{1,0:T(8,128)(2,1)S(1)}, u32[]{:S(2)}, u32[]{:S(2)}) collective-permute-start(bf16[32,1024]{1,0:T(8,128)(2,1)} %get-tuple-element.15), channel_id=1, source_target_pairs={{0,8},{8,0},{16,24},{24,16},{1,9},{9,1},{17,25},{25,17},{2,10},{10... | collective-permute-start | bytes 196616 | tf_op jit(solution)/shard_map/ppermute | solution.py:23
  128.8 7.4 %collective-permute-start.28 = (bf16[32,1024]{1,0:T(8,128)(2,1)}, bf16[32,1024]{1,0:T(8,128)(2,1)}, u32[]{:S(2)}, u32[]{:S(2)}) collective-permute-start(bf16[32,1024]{1,0:T(8,128)(2,1)} %get-tuple-element.17), channel_id=1, source_target_pairs={{0,16},{8,24},{16,0},{24,8},{1,17},{9,25},{17,1},{25,9},{2,18},{10... | collective-permute-start | bytes 196616 | tf_op jit(solution)/shard_map/ppermute | solution.py:23
  131.7 6.4 %collective-permute-start.29 = (bf16[32,1024]{1,0:T(8,128)(2,1)}, bf16[32,1024]{1,0:T(8,128)(2,1)}, u32[]{:S(2)}, u32[]{:S(2)}) collective-permute-start(bf16[32,1024]{1,0:T(8,128)(2,1)} %get-tuple-element.16), channel_id=1, source_target_pairs={{0,24},{8,16},{16,8},{24,0},{1,25},{9,17},{17,9},{25,1},{2,26},{10... | collective-permute-start | bytes 196616 | tf_op jit(solution)/shard_map/ppermute | solution.py:23
  (48 other events, 407.0 us)

commit v2 on v1

v2 whole, which is shorter than its diff:
```python
import jax
import jax.numpy as jnp
from jax import lax
from jax.experimental import pallas as pl
from jax.experimental.pallas import tpu as pltpu
from jax.sharding import PartitionSpec as P


TILE = 128
TILE_ROW = 4
LANES = 128


eps_norm = 1e-06


def silu_slope(values):
    sigma = jax.nn.sigmoid(values)
    return sigma * (1.0 + values * (1.0 - sigma))


def dot(a, b, ca=1, cb=0):
    return lax.dot_general(a, b, (((ca,), (cb,)), ((), ())), preferred_element_type=jnp.float32)


def swap(value, axis, size, mask):
    return lax.ppermute(value, axis, [(i, i ^ mask) for i in range(size)])


def call(body, outs, operands, scalars=0):
    flops = sum(2 * o.shape[0] * o.shape[1] * 1024 for o in outs)
    moved = sum(x.size * x.dtype.itemsize for x in list(operands) + list(outs))
    return pl.pallas_call(
        body,
        out_shape=outs,
        in_specs=[pl.BlockSpec(memory_space=pltpu.SMEM)] * scalars
        + [pl.BlockSpec(memory_space=pltpu.VMEM)] * (len(operands) - scalars),
        out_specs=[pl.BlockSpec(memory_space=pltpu.VMEM)] * len(outs),
        cost_estimate=pl.CostEstimate(flops=flops, bytes_accessed=moved, transcendentals=0),
    )(*operands)


def assemble(near, far, me, plain, turned):
    pieces = [piece for pair in zip(near, far) for piece in pair]
    count = len(pieces)
    rows, columns = pieces[0].shape
    if rows % LANES:
        both = jnp.stack(pieces, 0)[jnp.arange(count, dtype=jnp.int32) ^ me]
        both = both.reshape(count * rows, columns)
        return [both] * plain + [both.T] * turned

    def body(me_ref, *refs):
        for x in range(count):
            at = pl.ds(pl.multiple_of((me_ref[0] ^ x) * rows, rows), rows)
            value = refs[x][...]
            outs = list(refs[count:])
            if plain:
                outs.pop(0)[at, :] = value
            if turned:
                outs.pop(0)[:, at] = value.T

    outs = [jax.ShapeDtypeStruct((count * rows, columns), pieces[0].dtype)] * plain
    outs += [jax.ShapeDtypeStruct((columns, count * rows), pieces[0].dtype)] * turned
    return call(body, outs, [me[None]] + pieces, 1)


def last_step(counts, near, far, slope, weights):
    pieces = near + far

    def body(counts_ref, slope_ref, weights_ref, *refs):
        rows = jnp.concatenate([ref[...] for ref in refs[:-1]], 0)
        grad = (dot(counts_ref[...], rows) * slope_ref[...]).astype(jnp.bfloat16)
        refs[-1][...] = dot(grad, weights_ref[...]).astype(jnp.bfloat16)

    outs = [jax.ShapeDtypeStruct((counts.shape[0], weights.shape[1]), jnp.bfloat16)]
    return call(body, outs, [counts, slope, weights] + pieces)[0]


def own_counts(edge_codes, live_counts, source_ids, me, turn, own_rows, order):
    blocks = source_ids.shape[0] // TILE_ROW
    slots = edge_codes.shape[1]
    live = lax.broadcasted_iota(jnp.int32, edge_codes.shape, 1) < live_counts[:, None]
    source = source_ids[:, None] * TILE + edge_codes % TILE - me * own_rows
    source = jnp.where(live, source, -1)
    target = (edge_codes // TILE) ^ turn
    picked = jnp.asarray(order, jnp.int32) ^ me
    source = source.reshape(blocks, TILE_ROW * slots)[picked]
    target = target.reshape(blocks, TILE_ROW * slots)[picked]
    source_at = lax.broadcasted_iota(jnp.int32, (1, 1, own_rows), 2)
    target_at = lax.broadcasted_iota(jnp.int32, (1, 1, TILE), 2)
    source_hot = (source[:, :, None] == source_at).astype(jnp.bfloat16)
    target_hot = (target[:, :, None] == target_at).astype(jnp.bfloat16)
    counts = jnp.einsum("bet,bes->bts", target_hot, source_hot, preferred_element_type=jnp.float32)
    counts = counts.astype(jnp.bfloat16).reshape(-1, own_rows)
    return counts, counts.T


def make_shards(rels, devs):
    pairs = devs // 2
    evens = [2 * k for k in range(pairs)]
    odds = [2 * k + 1 for k in range(pairs)]

    def gather_dev(value):
        near = [value] + [swap(value, "dev", devs, 2 * k) for k in range(1, pairs)]
        return near, [swap(piece, "dev", devs, 1) for piece in near]

    def gather_rel(value):
        return [value] + [swap(value, "rel", rels, q) for q in range(1, rels)]

    def reduce_rel(value):
        rows = value.shape[0] // rels
        total = value[:rows]
        for q in range(1, rels):
            piece = value[q * rows : (q + 1) * rows].astype(jnp.bfloat16)
            total = total + swap(piece, "rel", rels, q).astype(jnp.float32)
        return total

    def shards(
        src_feat,
        rel_w_in,
        rel_w_out,
        tile_source,
        tile_edges,
        tile_count,
        target_feat,
        norm_gain,
        tgt_w_in,
        tgt_w_out,
        out_grad,
    ):
        me = lax.axis_index("dev")
        rel = lax.axis_index("rel")
        own_rows = src_feat[0]
        rows = own_rows.shape[0]
        shard = rel_w_in.shape[1]
        gain = norm_gain[None, :]
        order = jnp.asarray(evens + odds, jnp.int32) ^ me

        in_near, in_far = gather_dev(rel_w_in[0])
        out_near, out_far = gather_dev(rel_w_out[0])
        hidden_grad = dot(jnp.concatenate(gather_rel(out_grad), 0), tgt_w_out, 1, 1)
        sub = TILE // rels
        counts, counts_turned = own_counts(
            tile_edges[0], tile_count[0], tile_source[0], me, rel * sub, rows, evens + odds
        )
        columns = own_rows.reshape(rows, devs, shard)[:, order]
        hidden_pre = 0.0
        for k in range(pairs):
            hidden_pre = hidden_pre + dot(columns[:, k], in_near[k])
            hidden_pre = hidden_pre + dot(columns[:, pairs + k], in_far[k])
        hidden_pre, hidden_grad, counts, counts_turned = lax.optimization_barrier(
            (hidden_pre, hidden_grad, counts, counts_turned)
        )
        hidden = jax.nn.silu(hidden_pre).astype(jnp.bfloat16)

        half = pairs * TILE
        far = swap(dot(counts[half:], hidden).astype(jnp.bfloat16), "dev", devs, 1)
        near = dot(counts[:half], hidden) + far.astype(jnp.float32)
        total = near[:TILE]
        for k in range(1, pairs):
            piece = near[k * TILE : (k + 1) * TILE].astype(jnp.bfloat16)
            total = total + swap(piece, "dev", devs, 2 * k).astype(jnp.float32)
        out_full, out_turned = assemble(out_near, out_far, me, True, True)
        agg = reduce_rel(dot(total.astype(jnp.bfloat16), out_full))

        (in_turned,) = assemble(in_near, in_far, me, False, True)
        slope = silu_slope(hidden_pre)
        agg, in_turned, slope = lax.optimization_barrier((agg, in_turned, slope))
        inverse_norm = lax.rsqrt(jnp.mean(agg * agg, axis=1, keepdims=True) + eps_norm)
        normed = gather_rel((agg * inverse_norm * gain).astype(jnp.bfloat16))
        target_pre = dot(jnp.concatenate(normed, 0), tgt_w_in)
        grad_pre_t = (hidden_grad * silu_slope(target_pre)).astype(jnp.bfloat16)
        grad_normed = reduce_rel(dot(grad_pre_t, tgt_w_in, 1, 1))
        target_hidden = jax.nn.silu(target_pre).astype(jnp.bfloat16)
        scaled = grad_normed * gain
        mean_term = jnp.mean(agg * scaled, axis=1, keepdims=True)
        grad_agg = inverse_norm * (scaled - agg * inverse_norm * inverse_norm * mean_term)
        grad_agg = jnp.concatenate(gather_rel(grad_agg.astype(jnp.bfloat16)), 0)
        target_hidden, grad_agg = lax.optimization_barrier((target_hidden, grad_agg))

        back = dot(grad_agg, out_turned).astype(jnp.bfloat16)
        back_near, back_far = gather_dev(back)
        update = reduce_rel(dot(target_hidden, tgt_w_out))
        updated = (target_feat.astype(jnp.float32) + update).astype(jnp.bfloat16)
        grad_source = last_step(counts_turned, back_near, back_far, slope, in_turned)
        return (updated, grad_source[None])

    return shards


def solution(mesh):
    placed = (
        P("rel", "dev", None),
        P("rel", "dev", None),
        P("rel", "dev", None),
        P("rel", None),
        P("rel", None, None),
        P("rel", None),
        P(("dev", "rel"), None),
        P(),
        P(None, "rel"),
        P("rel", None),
        P(("dev", "rel"), None),
    )
    rels, devs = mesh.shape["rel"], mesh.shape["dev"]
    shards = make_shards(rels, devs)

    return jax.shard_map(
        shards,
        mesh=mesh,
        in_specs=placed,
        out_specs=(P(("dev", "rel"), None), P("rel", "dev", None)),
        check_vma=False,
    )
```

time: 147 us -> 129 us (0.88)
  waiting for transfers between devices: 58.3 us -> 45.1 us
  Pallas kernels: 0 us -> 12.4 us
  local copies, waits for them, and re-layouts: 15.7 us -> 8.63 us
  matrix products: 20.4 us -> 14.2 us
  other arithmetic: 8.69 us -> 3.33 us
  starting transfers between devices: 42 us -> 43.6 us
    ppermute x34 -> x43, waiting for transfers between devices: 58.3 us -> 45.1 us  [swap(): return lax.ppermute(value, axis, [(i, i ^ mask) for i in range(size)])]
    pallas_call x0 -> x3, Pallas kernels: none -> 12.4 us  [call(): pl.pallas_call(body, out_shape=outs, in_specs=[pl.BlockSpec(memory_space=...]
    dot_general x11 -> x16, matrix products: 19.1 us -> 12.1 us  [dot(): lax.dot_general(a, b, (((ca,), (cb,)), ((), ())), preferred_element_type=...]
    gather x5 -> x1, local copies, waits for them, and re-layouts: 6.57 us -> 0.65 us  [shards(): columns = own_rows.reshape(rows, devs, shard)[:, order]]
    concatenate x4 -> x1, other arithmetic: 3.27 us -> 0.02 us  [shards(): grad_agg = jnp.concatenate(gather_rel(grad_agg.astype(jnp.bfloat16)), 0)]
    ppermute x34 -> x43, starting transfers between devices: 42 us -> 43.6 us  [swap(): return lax.ppermute(value, axis, [(i, i ^ mask) for i in range(size)])]
    slice x3, local copies, waits for them, and re-layouts: 1.59 us -> 0.05 us  [reduce_rel(): piece = value[q * rows:(q + 1) * rows].astype(jnp.bfloat16)]
    unnamed x86 -> x72, local copies, waits for them, and re-layouts: 4.78 us -> 4.9 us
  transfers between devices with their start and end apart: 34 -> 43, of which waited for: 22 -> 22; matrix products, arithmetic and copies ran while one was open for 13% -> 13% of each run, Pallas kernels for 0% -> 6%
where the time goes in v2:
time: 129 us; the launch traced here: 128 us
  waiting for transfers between devices  45.1 us (35%)
  starting transfers between devices  43.6 us (34%)
  matrix products  14.2 us (11%)
  Pallas kernels  12.4 us (10%)
  local copies, waits for them, and re-layouts  8.63 us (7%)
  other arithmetic  3.33 us (3%)
    ppermute x43, waiting for transfers between devices, swap(): return lax.ppermute(value, axis, [(i, i ^ mask) for i in range(size)])  45.1 us
    ppermute x43, starting transfers between devices, swap(): return lax.ppermute(value, axis, [(i, i ^ mask) for i in range(size)])  43.6 us
    pallas_call x3, Pallas kernels, call(): pl.pallas_call(body, out_shape=outs, in_specs=[pl.BlockSpec(memory_space=...  12.4 us
    dot_general x16, matrix products, dot(): lax.dot_general(a, b, (((ca,), (cb,)), ((), ())), preferred_element_type=...  12.1 us
    unnamed x72, local copies, waits for them, and re-layouts  4.9 us
  transfers between devices with their start and end apart: 43, of which 22 were waited for; matrix products, arithmetic and copies ran while one was open for 13% of the time, Pallas kernels for 6%

profile of v2, /device:TPU:0, one launch (start us, length us, event | category | flops | bytes accessed | tf_op | source)
XLA Modules:
  0.0 128.3 jit_solution(5237748812401511017)
XLA Ops:
  0.7 4.0 %collective-permute-start.5 = (bf16[128,1024]{1,0:T(8,128)(2,1)}, bf16[128,1024]{1,0:T(8,128)(2,1)}, u32[]{:S(2)}, u32[]{:S(2)}) collective-permute-start(bf16[128,1024]{1,0:T(8,128)(2,1)} %bitcast.69), channel_id=1, source_target_pairs={{0,6},{1,7},{2,4},{3,5},{4,2},{5,3},{6,0},{7,1},{8,14},{9,15},{10,... | collective-permute-start | bytes 786440 | tf_op jit(solution)/shard_map/ppermute | solution.py:27
  5.2 3.6 %collective-permute-start.9 = (bf16[32,1024]{1,0:T(8,128)(2,1)}, bf16[32,1024]{1,0:T(8,128)(2,1)}, u32[]{:S(2)}, u32[]{:S(2)}) collective-permute-start(bf16[32,1024]{1,0:T(8,128)(2,1)} %param.23), channel_id=1, source_target_pairs={{0,24},{8,16},{16,8},{24,0},{1,25},{9,17},{17,9},{25,1},{2,26},{10... | collective-permute-start | bytes 196616 | tf_op jit(solution)/shard_map/ppermute | solution.py:27
  15.9 2.0 %fusion.4 = bf16[8,128,256]{2,1,0:T(8,128)(2,1)} fusion(s32[8,512]{1,0:T(8,128)S(1)} %gather_fusion.2, s32[8,512]{1,0:T(8,128)S(1)} %gather_fusion.1), kind=kOutput, calls=%fused_computation.16 | convolution fusion | flops 270270464 | bytes 557056 | tf_op jit(solution)/shard_map/bet,bes->bts/dot_general | solution.py:93
  19.5 2.5 %fusion.11 = f32[128,512]{1,0:T(8,128)} fusion(bf16[512,1024]{1,0:T(8,128)(2,1)} %param.22, bf16[32,1024]{1,0:T(8,128)(2,1)} %collective-permute-done.9, bf16[32,1024]{1,0:T(8,128)(2,1)} %collective-permute-done.8, bf16[32,1024]{1,0:T(8,128)(2,1)} %collective-permute-done.7, bf16[32,1024]{1,0:T(8,128)(2,1)S(1)} %copy-done.31), kind=kOutput, calls=%fused_computation.27 | convolution fusion | flops 135266304 | bytes 1572864 | tf_op jit(solution)/shard_map/dot_general | solution.py:23
  33.6 5.7 %collective-permute-done.15.refs_2_ = bf16[128,1024]{1,0:T(8,128)(2,1)S(1)} collective-permute-done((bf16[128,1024]{1,0:T(8,128)(2,1)S(1)}, bf16[128,1024]{1,0:T(8,128)(2,1)S(1)}, u32[]{:S(2)}, u32[]{:S(2)}) %collective-permute-start.15) | collective-permute-done | bytes 262176 | tf_op jit(solution)/shard_map/ppermute | solution.py:27
  39.3 6.2 %collective-permute-done.17.refs_4_ = bf16[128,1024]{1,0:T(8,128)(2,1)S(1)} collective-permute-done((bf16[128,1024]{1,0:T(8,128)(2,1)S(1)}, bf16[128,1024]{1,0:T(8,128)(2,1)S(1)}, u32[]{:S(2)}, u32[]{:S(2)}) %collective-permute-start.17) | collective-permute-done | bytes 262176 | tf_op jit(solution)/shard_map/ppermute | solution.py:27
  48.5 4.2 %shard_map.140 = (bf16[1024,1024]{1,0:T(8,128)(2,1)}, bf16[1024,1024]{1,0:T(8,128)(2,1)}) custom-call(s32[1]{0:T(128)} %bitcast.16.me_ref, bf16[128,1024]{1,0:T(8,128)(2,1)} %bitcast.74, bf16[128,1024]{1,0:T(8,128)(2,1)} %copy-done.27, bf16[128,1024]{1,0:T(8,128)(2,1)} %copy-done.24, bf16[128,1024]{1,0:T(8,128)(2,1)} %copy-done.28, ...), custom_call_target="tpu_custom_call" | custom-call | flops 4294967296 | bytes 6291460 | tf_op jit(solution)/shard_map/pallas_call | solution.py:33
  56.0 2.0 %collective-permute-start.11 = (bf16[128,1024]{1,0:T(8,128)(2,1)S(1)}, bf16[128,1024]{1,0:T(8,128)(2,1)S(1)}, u32[]{:S(2)}, u32[]{:S(2)}) collective-permute-start(bf16[128,1024]{1,0:T(8,128)(2,1)S(1)} %get-tuple-element.24), channel_id=1, source_target_pairs={{0,2},{1,3},{2,0},{3,1},{4,6},{5,7},{6,4},{7,5},{8,10},{9,11},{10,... | collective-permute-start | bytes 786440 | tf_op jit(solution)/shard_map/ppermute | solution.py:27
  59.4 5.3 %collective-permute-done.13 = bf16[128,1024]{1,0:T(8,128)(2,1)S(1)} collective-permute-done((bf16[128,1024]{1,0:T(8,128)(2,1)S(1)}, bf16[128,1024]{1,0:T(8,128)(2,1)S(1)}, u32[]{:S(2)}, u32[]{:S(2)}) %collective-permute-start.13) | collective-permute-done | bytes 262176 | tf_op jit(solution)/shard_map/ppermute | solution.py:27
  64.7 4.0 %collective-permute-done.12 = bf16[128,1024]{1,0:T(8,128)(2,1)S(1)} collective-permute-done((bf16[128,1024]{1,0:T(8,128)(2,1)S(1)}, bf16[128,1024]{1,0:T(8,128)(2,1)S(1)}, u32[]{:S(2)}, u32[]{:S(2)}) %collective-permute-start.12) | collective-permute-done | bytes 262176 | tf_op jit(solution)/shard_map/ppermute | solution.py:27
  69.5 3.7 %collective-permute-start.23 = (bf16[32,1024]{1,0:T(8,128)(2,1)S(1)}, bf16[32,1024]{1,0:T(8,128)(2,1)S(1)}, u32[]{:S(2)}, u32[]{:S(2)}) collective-permute-start(bf16[32,1024]{1,0:T(8,128)(2,1)S(1)} %get-tuple-element.34), channel_id=1, source_target_pairs={{0,24},{8,16},{16,8},{24,0},{1,25},{9,17},{17,9},{25,1},{2,26},{10... | collective-permute-start | bytes 196616 | tf_op jit(solution)/shard_map/ppermute | solution.py:27
  73.9 3.6 %shard_map.141.weights_ref = bf16[1024,1024]{1,0:T(8,128)(2,1)} custom-call(s32[1]{0:T(128)} %bitcast.16.me_ref, bf16[128,1024]{1,0:T(8,128)(2,1)} %bitcast.73, bf16[128,1024]{1,0:T(8,128)(2,1)} %copy-done.8, bf16[128,1024]{1,0:T(8,128)(2,1)} %copy-done.6, bf16[128,1024]{1,0:T(8,128)(2,1)} %copy-done.18, bf16[128,1024]{1,0:T(8,128)(2,1)} %copy-done.17, ...), custom_call_target="tpu_custom_call" | custom-call | flops 2147483648 | bytes 4194308 | tf_op jit(solution)/shard_map/pallas_call | solution.py:33
  78.8 2.7 %collective-permute-start.26 = (bf16[32,1024]{1,0:T(8,128)(2,1)S(1)}, bf16[32,1024]{1,0:T(8,128)(2,1)S(1)}, u32[]{:S(2)}, u32[]{:S(2)}) collective-permute-start(bf16[32,1024]{1,0:T(8,128)(2,1)S(1)} %multiply_convert_fusion.5), channel_id=1, source_target_pairs={{0,24},{8,16},{16,8},{24,0},{1,25},{9,17},{17,9},{25,1},{2,26},{10... | collective-permute-start | bytes 196616 | tf_op jit(solution)/shard_map/ppermute | solution.py:27
  83.3 2.3 %collective-permute-done.26 = bf16[32,1024]{1,0:T(8,128)(2,1)S(1)} collective-permute-done((bf16[32,1024]{1,0:T(8,128)(2,1)S(1)}, bf16[32,1024]{1,0:T(8,128)(2,1)S(1)}, u32[]{:S(2)}, u32[]{:S(2)}) %collective-permute-start.26) | collective-permute-done | bytes 65568 | tf_op jit(solution)/shard_map/ppermute | solution.py:27
  88.0 2.2 %collective-permute-start.29 = (bf16[32,1024]{1,0:T(8,128)(2,1)S(1)}, bf16[32,1024]{1,0:T(8,128)(2,1)S(1)}, u32[]{:S(2)}, u32[]{:S(2)}) collective-permute-start(bf16[32,1024]{1,0:T(8,128)(2,1)S(1)} %get-tuple-element.31), channel_id=1, source_target_pairs={{0,24},{8,16},{16,8},{24,0},{1,25},{9,17},{17,9},{25,1},{2,26},{10... | collective-permute-start | bytes 196616 | tf_op jit(solution)/shard_map/ppermute | solution.py:27
  90.2 2.2 %collective-permute-start.27 = (bf16[32,1024]{1,0:T(8,128)(2,1)S(1)}, bf16[32,1024]{1,0:T(8,128)(2,1)S(1)}, u32[]{:S(2)}, u32[]{:S(2)}) collective-permute-start(bf16[32,1024]{1,0:T(8,128)(2,1)S(1)} %get-tuple-element.30), channel_id=1, source_target_pairs={{0,8},{8,0},{16,24},{24,16},{1,9},{9,1},{17,25},{25,17},{2,10},{10... | collective-permute-start | bytes 196616 | tf_op jit(solution)/shard_map/ppermute | solution.py:27
  92.4 2.1 %collective-permute-done.29 = bf16[32,1024]{1,0:T(8,128)(2,1)S(1)} collective-permute-done((bf16[32,1024]{1,0:T(8,128)(2,1)S(1)}, bf16[32,1024]{1,0:T(8,128)(2,1)S(1)}, u32[]{:S(2)}, u32[]{:S(2)}) %collective-permute-start.29) | collective-permute-done | bytes 65568 | tf_op jit(solution)/shard_map/ppermute | solution.py:27
  96.7 2.2 %collective-permute-start.32 = (bf16[32,1024]{1,0:T(8,128)(2,1)S(1)}, bf16[32,1024]{1,0:T(8,128)(2,1)S(1)}, u32[]{:S(2)}, u32[]{:S(2)}) collective-permute-start(bf16[32,1024]{1,0:T(8,128)(2,1)S(1)} %multiply_convert_fusion.4), channel_id=1, source_target_pairs={{0,24},{8,16},{16,8},{24,0},{1,25},{9,17},{17,9},{25,1},{2,26},{10... | collective-permute-start | bytes 196616 | tf_op jit(solution)/shard_map/ppermute | solution.py:27
  98.9 2.2 %collective-permute-start.30 = (bf16[32,1024]{1,0:T(8,128)(2,1)S(1)}, bf16[32,1024]{1,0:T(8,128)(2,1)S(1)}, u32[]{:S(2)}, u32[]{:S(2)}) collective-permute-start(bf16[32,1024]{1,0:T(8,128)(2,1)S(1)} %multiply_convert_fusion.4), channel_id=1, source_target_pairs={{0,8},{8,0},{16,24},{24,16},{1,9},{9,1},{17,25},{25,17},{2,10},{10... | collective-permute-start | bytes 196616 | tf_op jit(solution)/shard_map/ppermute | solution.py:27
  101.1 2.2 %collective-permute-done.32 = bf16[32,1024]{1,0:T(8,128)(2,1)S(1)} collective-permute-done((bf16[32,1024]{1,0:T(8,128)(2,1)S(1)}, bf16[32,1024]{1,0:T(8,128)(2,1)S(1)}, u32[]{:S(2)}, u32[]{:S(2)}) %collective-permute-start.32) | collective-permute-done | bytes 65568 | tf_op jit(solution)/shard_map/ppermute | solution.py:27
  109.5 2.0 %collective-permute-start.35 = (bf16[32,1024]{1,0:T(8,128)(2,1)S(1)}, bf16[32,1024]{1,0:T(8,128)(2,1)S(1)}, u32[]{:S(2)}, u32[]{:S(2)}) collective-permute-start(bf16[32,1024]{1,0:T(8,128)(2,1)S(1)} %get-tuple-element.28), channel_id=1, source_target_pairs={{0,24},{8,16},{16,8},{24,0},{1,25},{9,17},{17,9},{25,1},{2,26},{10... | collective-permute-start | bytes 196616 | tf_op jit(solution)/shard_map/ppermute | solution.py:27
  111.6 4.2 %collective-permute-done.35 = bf16[32,1024]{1,0:T(8,128)(2,1)S(1)} collective-permute-done((bf16[32,1024]{1,0:T(8,128)(2,1)S(1)}, bf16[32,1024]{1,0:T(8,128)(2,1)S(1)}, u32[]{:S(2)}, u32[]{:S(2)}) %collective-permute-start.35) | collective-permute-done | bytes 65568 | tf_op jit(solution)/shard_map/ppermute | solution.py:27
  118.4 2.3 %collective-permute-done.37.refs_2_ = bf16[128,1024]{1,0:T(8,128)(2,1)S(1)} collective-permute-done((bf16[128,1024]{1,0:T(8,128)(2,1)S(1)}, bf16[128,1024]{1,0:T(8,128)(2,1)S(1)}, u32[]{:S(2)}, u32[]{:S(2)}) %collective-permute-start.37) | collective-permute-done | bytes 262176 | tf_op jit(solution)/shard_map/ppermute | solution.py:27
  123.6 4.6 %shard_map.142 = bf16[256,1024]{1,0:T(8,128)(2,1)} custom-call(bf16[256,1024]{1,0:T(8,128)(2,1)} %bitcast.57, f32[256,1024]{1,0:T(8,128)} %add_multiply_fusion.slope_ref, bf16[1024,1024]{1,0:T(8,128)(2,1)} %shard_map.141.weights_ref, bf16[128,1024]{1,0:T(8,128)(2,1)} %copy-done.4, bf16[128,1024]{1,0:T(8,128)(2,1)} %copy-done.10, ...), custom_call_target="tpu_custom_call" | custom-call | flops 536870912 | bytes 6291456 | tf_op jit(solution)/shard_map/pallas_call | solution.py:33
  (184 shorter events, 49.0 us)
Async XLA Ops:
  0.7 21.9 %collective-permute-start.5 = (bf16[128,1024]{1,0:T(8,128)(2,1)}, bf16[128,1024]{1,0:T(8,128)(2,1)}, u32[]{:S(2)}, u32[]{:S(2)}) collective-permute-start(bf16[128,1024]{1,0:T(8,128)(2,1)} %bitcast.69), channel_id=1, source_target_pairs={{0,6},{1,7},{2,4},{3,5},{4,2},{5,3},{6,0},{7,1},{8,14},{9,15},{10,... | collective-permute-start | bytes 786440 | tf_op jit(solution)/shard_map/ppermute | solution.py:27
  4.6 17.4 %collective-permute-start.1 = (bf16[128,1024]{1,0:T(8,128)(2,1)}, bf16[128,1024]{1,0:T(8,128)(2,1)S(1)}, u32[]{:S(2)}, u32[]{:S(2)}) collective-permute-start(bf16[128,1024]{1,0:T(8,128)(2,1)} %bitcast.70), channel_id=1, source_target_pairs={{0,2},{1,3},{2,0},{3,1},{4,6},{5,7},{6,4},{7,5},{8,10},{9,11},{10,... | collective-permute-start | bytes 786440 | tf_op jit(solution)/shard_map/ppermute | solution.py:27
  5.2 14.0 %collective-permute-start.9 = (bf16[32,1024]{1,0:T(8,128)(2,1)}, bf16[32,1024]{1,0:T(8,128)(2,1)}, u32[]{:S(2)}, u32[]{:S(2)}) collective-permute-start(bf16[32,1024]{1,0:T(8,128)(2,1)} %param.23), channel_id=1, source_target_pairs={{0,24},{8,16},{16,8},{24,0},{1,25},{9,17},{17,9},{25,1},{2,26},{10... | collective-permute-start | bytes 196616 | tf_op jit(solution)/shard_map/ppermute | solution.py:27
  8.8 10.7 %collective-permute-start.8 = (bf16[32,1024]{1,0:T(8,128)(2,1)}, bf16[32,1024]{1,0:T(8,128)(2,1)}, u32[]{:S(2)}, u32[]{:S(2)}) collective-permute-start(bf16[32,1024]{1,0:T(8,128)(2,1)} %param.23), channel_id=1, source_target_pairs={{0,16},{8,24},{16,0},{24,8},{1,17},{9,25},{17,1},{25,9},{2,18},{10... | collective-permute-start | bytes 196616 | tf_op jit(solution)/shard_map/ppermute | solution.py:27
  8.8 10.7 %collective-permute-start.7 = (bf16[32,1024]{1,0:T(8,128)(2,1)}, bf16[32,1024]{1,0:T(8,128)(2,1)}, u32[]{:S(2)}, u32[]{:S(2)}) collective-permute-start(bf16[32,1024]{1,0:T(8,128)(2,1)} %param.23), channel_id=1, source_target_pairs={{0,8},{8,0},{16,24},{24,16},{1,9},{9,1},{17,25},{25,17},{2,10},{10... | collective-permute-start | bytes 196616 | tf_op jit(solution)/shard_map/ppermute | solution.py:27
  19.2 7.0 %collective-permute-start.3 = (bf16[128,1024]{1,0:T(8,128)(2,1)}, bf16[128,1024]{1,0:T(8,128)(2,1)S(1)}, u32[]{:S(2)}, u32[]{:S(2)}) collective-permute-start(bf16[128,1024]{1,0:T(8,128)(2,1)} %bitcast.71), channel_id=1, source_target_pairs={{0,4},{1,5},{2,6},{3,7},{4,0},{5,1},{6,2},{7,3},{8,12},{9,13},{10,... | collective-permute-start | bytes 786440 | tf_op jit(solution)/shard_map/ppermute | solution.py:27
  30.0 22.7 %collective-permute-start.10 = (bf16[512,1024]{1,0:T(8,128)(2,1)}, bf16[512,1024]{1,0:T(8,128)(2,1)}, u32[]{:S(2)}, u32[]{:S(2)}) collective-permute-start(bf16[512,1024]{1,0:T(8,128)(2,1)} %convolution_convert_fusion), channel_id=1, source_target_pairs={{0,1},{1,0},{2,3},{3,2},{4,5},{5,4},{6,7},{7,6},{8,9},{9,8},{10,11... | collective-permute-start | bytes 3145736 | tf_op jit(solution)/shard_map/ppermute | solution.py:27
  30.1 9.2 %collective-permute-start.15 = (bf16[128,1024]{1,0:T(8,128)(2,1)S(1)}, bf16[128,1024]{1,0:T(8,128)(2,1)S(1)}, u32[]{:S(2)}, u32[]{:S(2)}) collective-permute-start(bf16[128,1024]{1,0:T(8,128)(2,1)S(1)} %bitcast.75), channel_id=1, source_target_pairs={{0,2},{1,3},{2,0},{3,1},{4,6},{5,7},{6,4},{7,5},{8,10},{9,11},{10,... | collective-permute-start | bytes 786440 | tf_op jit(solution)/shard_map/ppermute | solution.py:27
  31.6 13.9 %collective-permute-start.17 = (bf16[128,1024]{1,0:T(8,128)(2,1)S(1)}, bf16[128,1024]{1,0:T(8,128)(2,1)S(1)}, u32[]{:S(2)}, u32[]{:S(2)}) collective-permute-start(bf16[128,1024]{1,0:T(8,128)(2,1)S(1)} %bitcast.76), channel_id=1, source_target_pairs={{0,4},{1,5},{2,6},{3,7},{4,0},{5,1},{6,2},{7,3},{8,12},{9,13},{10,... | collective-permute-start | bytes 786440 | tf_op jit(solution)/shard_map/ppermute | solution.py:27
  32.8 12.7 %collective-permute-start.19 = (bf16[128,1024]{1,0:T(8,128)(2,1)S(1)}, bf16[128,1024]{1,0:T(8,128)(2,1)S(1)}, u32[]{:S(2)}, u32[]{:S(2)}) collective-permute-start(bf16[128,1024]{1,0:T(8,128)(2,1)S(1)} %bitcast.77), channel_id=1, source_target_pairs={{0,6},{1,7},{2,4},{3,5},{4,2},{5,3},{6,0},{7,1},{8,14},{9,15},{10,... | collective-permute-start | bytes 786440 | tf_op jit(solution)/shard_map/ppermute | solution.py:27
  33.6 12.5 %collective-permute-start.14 = (bf16[128,1024]{1,0:T(8,128)(2,1)S(1)}, bf16[128,1024]{1,0:T(8,128)(2,1)S(1)}, u32[]{:S(2)}, u32[]{:S(2)}) collective-permute-start(bf16[128,1024]{1,0:T(8,128)(2,1)S(1)} %bitcast.78), channel_id=1, source_target_pairs={{0,1},{1,0},{2,3},{3,2},{4,5},{5,4},{6,7},{7,6},{8,9},{9,8},{10,11... | collective-permute-start | bytes 786440 | tf_op jit(solution)/shard_map/ppermute | solution.py:27
  39.3 6.8 %collective-permute-start.16 = (bf16[128,1024]{1,0:T(8,128)(2,1)S(1)}, bf16[128,1024]{1,0:T(8,128)(2,1)S(1)}, u32[]{:S(2)}, u32[]{:S(2)}) collective-permute-start(bf16[128,1024]{1,0:T(8,128)(2,1)S(1)} %collective-permute-done.15.refs_2_), channel_id=1, source_target_pairs={{0,1},{1,0},{2,3},{3,2},{4,5},{5,4},{6,7},{7,6},{8,9},{9,8},{10,11... | collective-permute-start | bytes 786440 | tf_op jit(solution)/shard_map/ppermute | solution.py:27
  54.5 10.2 %collective-permute-start.13 = (bf16[128,1024]{1,0:T(8,128)(2,1)S(1)}, bf16[128,1024]{1,0:T(8,128)(2,1)S(1)}, u32[]{:S(2)}, u32[]{:S(2)}) collective-permute-start(bf16[128,1024]{1,0:T(8,128)(2,1)S(1)} %get-tuple-element.25), channel_id=1, source_target_pairs={{0,6},{1,7},{2,4},{3,5},{4,2},{5,3},{6,0},{7,1},{8,14},{9,15},{10,... | collective-permute-start | bytes 786440 | tf_op jit(solution)/shard_map/ppermute | solution.py:27
  55.1 13.7 %collective-permute-start.12 = (bf16[128,1024]{1,0:T(8,128)(2,1)S(1)}, bf16[128,1024]{1,0:T(8,128)(2,1)S(1)}, u32[]{:S(2)}, u32[]{:S(2)}) collective-permute-start(bf16[128,1024]{1,0:T(8,128)(2,1)S(1)} %get-tuple-element.26), channel_id=1, source_target_pairs={{0,4},{1,5},{2,6},{3,7},{4,0},{5,1},{6,2},{7,3},{8,12},{9,13},{10,... | collective-permute-start | bytes 786440 | tf_op jit(solution)/shard_map/ppermute | solution.py:27
  56.0 13.0 %collective-permute-start.11 = (bf16[128,1024]{1,0:T(8,128)(2,1)S(1)}, bf16[128,1024]{1,0:T(8,128)(2,1)S(1)}, u32[]{:S(2)}, u32[]{:S(2)}) collective-permute-start(bf16[128,1024]{1,0:T(8,128)(2,1)S(1)} %get-tuple-element.24), channel_id=1, source_target_pairs={{0,2},{1,3},{2,0},{3,1},{4,6},{5,7},{6,4},{7,5},{8,10},{9,11},{10,... | collective-permute-start | bytes 786440 | tf_op jit(solution)/shard_map/ppermute | solution.py:27
  69.5 8.0 %collective-permute-start.23 = (bf16[32,1024]{1,0:T(8,128)(2,1)S(1)}, bf16[32,1024]{1,0:T(8,128)(2,1)S(1)}, u32[]{:S(2)}, u32[]{:S(2)}) collective-permute-start(bf16[32,1024]{1,0:T(8,128)(2,1)S(1)} %get-tuple-element.34), channel_id=1, source_target_pairs={{0,24},{8,16},{16,8},{24,0},{1,25},{9,17},{17,9},{25,1},{2,26},{10... | collective-permute-start | bytes 196616 | tf_op jit(solution)/shard_map/ppermute | solution.py:27
  78.8 6.8 %collective-permute-start.26 = (bf16[32,1024]{1,0:T(8,128)(2,1)S(1)}, bf16[32,1024]{1,0:T(8,128)(2,1)S(1)}, u32[]{:S(2)}, u32[]{:S(2)}) collective-permute-start(bf16[32,1024]{1,0:T(8,128)(2,1)S(1)} %multiply_convert_fusion.5), channel_id=1, source_target_pairs={{0,24},{8,16},{16,8},{24,0},{1,25},{9,17},{17,9},{25,1},{2,26},{10... | collective-permute-start | bytes 196616 | tf_op jit(solution)/shard_map/ppermute | solution.py:27
  88.0 6.6 %collective-permute-start.29 = (bf16[32,1024]{1,0:T(8,128)(2,1)S(1)}, bf16[32,1024]{1,0:T(8,128)(2,1)S(1)}, u32[]{:S(2)}, u32[]{:S(2)}) collective-permute-start(bf16[32,1024]{1,0:T(8,128)(2,1)S(1)} %get-tuple-element.31), channel_id=1, source_target_pairs={{0,24},{8,16},{16,8},{24,0},{1,25},{9,17},{17,9},{25,1},{2,26},{10... | collective-permute-start | bytes 196616 | tf_op jit(solution)/shard_map/ppermute | solution.py:27
  96.7 6.6 %collective-permute-start.32 = (bf16[32,1024]{1,0:T(8,128)(2,1)S(1)}, bf16[32,1024]{1,0:T(8,128)(2,1)S(1)}, u32[]{:S(2)}, u32[]{:S(2)}) collective-permute-start(bf16[32,1024]{1,0:T(8,128)(2,1)S(1)} %multiply_convert_fusion.4), channel_id=1, source_target_pairs={{0,24},{8,16},{16,8},{24,0},{1,25},{9,17},{17,9},{25,1},{2,26},{10... | collective-permute-start | bytes 196616 | tf_op jit(solution)/shard_map/ppermute | solution.py:27
  105.6 12.2 %collective-permute-start.36 = (bf16[128,1024]{1,0:T(8,128)(2,1)S(1)}, bf16[128,1024]{1,0:T(8,128)(2,1)S(1)}, u32[]{:S(2)}, u32[]{:S(2)}) collective-permute-start(bf16[128,1024]{1,0:T(8,128)(2,1)S(1)} %convolution_convert_fusion.1.refs_0_), channel_id=1, source_target_pairs={{0,2},{1,3},{2,0},{3,1},{4,6},{5,7},{6,4},{7,5},{8,10},{9,11},{10,... | collective-permute-start | bytes 786440 | tf_op jit(solution)/shard_map/ppermute | solution.py:27
  107.1 13.6 %collective-permute-start.37 = (bf16[128,1024]{1,0:T(8,128)(2,1)S(1)}, bf16[128,1024]{1,0:T(8,128)(2,1)S(1)}, u32[]{:S(2)}, u32[]{:S(2)}) collective-permute-start(bf16[128,1024]{1,0:T(8,128)(2,1)S(1)} %convolution_convert_fusion.1.refs_0_), channel_id=1, source_target_pairs={{0,4},{1,5},{2,6},{3,7},{4,0},{5,1},{6,2},{7,3},{8,12},{9,13},{10,... | collective-permute-start | bytes 786440 | tf_op jit(solution)/shard_map/ppermute | solution.py:27
  108.1 12.5 %collective-permute-start.38 = (bf16[128,1024]{1,0:T(8,128)(2,1)S(1)}, bf16[128,1024]{1,0:T(8,128)(2,1)S(1)}, u32[]{:S(2)}, u32[]{:S(2)}) collective-permute-start(bf16[128,1024]{1,0:T(8,128)(2,1)S(1)} %convolution_convert_fusion.1.refs_0_), channel_id=1, source_target_pairs={{0,6},{1,7},{2,4},{3,5},{4,2},{5,3},{6,0},{7,1},{8,14},{9,15},{10,... | collective-permute-start | bytes 786440 | tf_op jit(solution)/shard_map/ppermute | solution.py:27
  109.5 6.2 %collective-permute-start.35 = (bf16[32,1024]{1,0:T(8,128)(2,1)S(1)}, bf16[32,1024]{1,0:T(8,128)(2,1)S(1)}, u32[]{:S(2)}, u32[]{:S(2)}) collective-permute-start(bf16[32,1024]{1,0:T(8,128)(2,1)S(1)} %get-tuple-element.28), channel_id=1, source_target_pairs={{0,24},{8,16},{16,8},{24,0},{1,25},{9,17},{17,9},{25,1},{2,26},{10... | collective-permute-start | bytes 196616 | tf_op jit(solution)/shard_map/ppermute | solution.py:27
  111.6 6.3 %collective-permute-start.34 = (bf16[32,1024]{1,0:T(8,128)(2,1)S(1)}, bf16[32,1024]{1,0:T(8,128)(2,1)S(1)}, u32[]{:S(2)}, u32[]{:S(2)}) collective-permute-start(bf16[32,1024]{1,0:T(8,128)(2,1)S(1)} %get-tuple-element.29), channel_id=1, source_target_pairs={{0,16},{8,24},{16,0},{24,8},{1,17},{9,25},{17,1},{25,9},{2,18},{10... | collective-permute-start | bytes 196616 | tf_op jit(solution)/shard_map/ppermute | solution.py:27
  (54 other events, 370.8 us)

commit v3 on v2

--- a/solution.py
+++ b/solution.py
@@ -64,35 +64,47 @@
     return call(body, outs, [me[None]] + pieces, 1)
 
 
-def last_step(counts, near, far, slope, weights):
-    pieces = near + far
-
-    def body(counts_ref, slope_ref, weights_ref, *refs):
-        rows = jnp.concatenate([ref[...] for ref in refs[:-1]], 0)
-        grad = (dot(counts_ref[...], rows) * slope_ref[...]).astype(jnp.bfloat16)
-        refs[-1][...] = dot(grad, weights_ref[...]).astype(jnp.bfloat16)
-
-    outs = [jax.ShapeDtypeStruct((counts.shape[0], weights.shape[1]), jnp.bfloat16)]
-    return call(body, outs, [counts, slope, weights] + pieces)[0]
-
-
-def own_counts(edge_codes, live_counts, source_ids, me, turn, own_rows, order):
-    blocks = source_ids.shape[0] // TILE_ROW
+def prepare(edge_codes, live_counts, source_ids, rows, me, turn, order, shard):
+    own, width = rows.shape
     slots = edge_codes.shape[1]
-    live = lax.broadcasted_iota(jnp.int32, edge_codes.shape, 1) < live_counts[:, None]
-    source = source_ids[:, None] * TILE + edge_codes % TILE - me * own_rows
-    source = jnp.where(live, source, -1)
-    target = (edge_codes // TILE) ^ turn
-    picked = jnp.asarray(order, jnp.int32) ^ me
-    source = source.reshape(blocks, TILE_ROW * slots)[picked]
-    target = target.reshape(blocks, TILE_ROW * slots)[picked]
-    source_at = lax.broadcasted_iota(jnp.int32, (1, 1, own_rows), 2)
-    target_at = lax.broadcasted_iota(jnp.int32, (1, 1, TILE), 2)
-    source_hot = (source[:, :, None] == source_at).astype(jnp.bfloat16)
-    target_hot = (target[:, :, None] == target_at).astype(jnp.bfloat16)
-    counts = jnp.einsum("bet,bes->bts", target_hot, source_hot, preferred_element_type=jnp.float32)
-    counts = counts.astype(jnp.bfloat16).reshape(-1, own_rows)
-    return counts, counts.T
+    count = len(order)
+    inside = shard % LANES == 0
+
+    def body(scalar_ref, source_ref, live_ref, edge_ref, rows_ref, counts_ref, turned_ref, *rest):
+        at, twist = scalar_ref[0], scalar_ref[1]
+        slot = lax.broadcasted_iota(jnp.int32, (1, slots), 1)
+        source_at = lax.broadcasted_iota(jnp.int32, (own, TILE_ROW * slots), 0)
+        target_at = lax.broadcasted_iota(jnp.int32, (TILE, TILE_ROW * slots), 0)
+        for i, x in enumerate(order):
+            sources, targets = [], []
+            for j in range(TILE_ROW):
+                tile = (at ^ x) * TILE_ROW + j
+                codes = edge_ref[pl.ds(tile, 1), :]
+                source = source_ref[tile] * TILE + (codes & (TILE - 1)) - at * own
+                sources.append(jnp.where(slot < live_ref[tile], source, -1))
+                targets.append((codes // TILE) ^ twist)
+            source_hot = (jnp.concatenate(sources, 1) == source_at).astype(jnp.float32)
+            target_hot = (jnp.concatenate(targets, 1) == target_at).astype(jnp.float32)
+            source_hot = source_hot.astype(jnp.bfloat16)
+            target_hot = target_hot.astype(jnp.bfloat16)
+            block = pl.ds(i * TILE, TILE)
+            counts_ref[block, :] = dot(target_hot, source_hot, 1, 1).astype(jnp.bfloat16)
+            turned_ref[:, block] = dot(source_hot, target_hot, 1, 1).astype(jnp.bfloat16)
+            if inside:
+                start = pl.multiple_of((at ^ x) * shard, shard)
+                rest[0][:, i * shard : (i + 1) * shard] = rows_ref[:, pl.ds(start, shard)]
+
+    outs = [
+        jax.ShapeDtypeStruct((count * TILE, own), jnp.bfloat16),
+        jax.ShapeDtypeStruct((own, count * TILE), jnp.bfloat16),
+    ]
+    outs += [jax.ShapeDtypeStruct((own, width), rows.dtype)] * inside
+    operands = [jnp.stack([me, turn]), source_ids, live_counts, edge_codes, rows]
+    results = call(body, outs, operands, 3)
+    if not inside:
+        picked = jnp.asarray(order, jnp.int32) ^ me
+        results = [*results, rows.reshape(own, count, shard)[:, picked].reshape(own, width)]
+    return results
 
 
 def make_shards(rels, devs):
@@ -131,27 +143,27 @@
         me = lax.axis_index("dev")
         rel = lax.axis_index("rel")
         own_rows = src_feat[0]
-        rows = own_rows.shape[0]
         shard = rel_w_in.shape[1]
         gain = norm_gain[None, :]
-        order = jnp.asarray(evens + odds, jnp.int32) ^ me
 
         in_near, in_far = gather_dev(rel_w_in[0])
         out_near, out_far = gather_dev(rel_w_out[0])
-        hidden_grad = dot(jnp.concatenate(gather_rel(out_grad), 0), tgt_w_out, 1, 1)
-        sub = TILE // rels
-        counts, counts_turned = own_counts(
-            tile_edges[0], tile_count[0], tile_source[0], me, rel * sub, rows, evens + odds
+        shared_grad = gather_rel(out_grad)
+        counts, counts_turned, columns = prepare(
+            tile_edges[0],
+            tile_count[0],
+            tile_source[0],
+            own_rows,
+            me,
+            rel * (TILE // rels),
+            evens + odds,
+            shard,
         )
-        columns = own_rows.reshape(rows, devs, shard)[:, order]
         hidden_pre = 0.0
         for k in range(pairs):
-            hidden_pre = hidden_pre + dot(columns[:, k], in_near[k])
-            hidden_pre = hidden_pre + dot(columns[:, pairs + k], in_far[k])
-        hidden_pre, hidden_grad, counts, counts_turned = lax.optimization_barrier(
-            (hidden_pre, hidden_grad, counts, counts_turned)
-        )
-        hidden = jax.nn.silu(hidden_pre).astype(jnp.bfloat16)
+            for at, piece in ((k, in_near[k]), (pairs + k, in_far[k])):
+                hidden_pre = hidden_pre + dot(columns[:, at * shard : (at + 1) * shard], piece)
+        hidden = lax.optimization_barrier(jax.nn.silu(hidden_pre).astype(jnp.bfloat16))
 
         half = pairs * TILE
         far = swap(dot(counts[half:], hidden).astype(jnp.bfloat16), "dev", devs, 1)
@@ -165,7 +177,10 @@
 
         (in_turned,) = assemble(in_near, in_far, me, False, True)
         slope = silu_slope(hidden_pre)
-        agg, in_turned, slope = lax.optimization_barrier((agg, in_turned, slope))
+        hidden_grad = dot(jnp.concatenate(shared_grad, 0), tgt_w_out, 1, 1)
+        agg, in_turned, slope, hidden_grad = lax.optimization_barrier(
+            (agg, in_turned, slope, hidden_grad)
+        )
         inverse_norm = lax.rsqrt(jnp.mean(agg * agg, axis=1, keepdims=True) + eps_norm)
         normed = gather_rel((agg * inverse_norm * gain).astype(jnp.bfloat16))
         target_pre = dot(jnp.concatenate(normed, 0), tgt_w_in)
@@ -182,8 +197,13 @@
         back_near, back_far = gather_dev(back)
         update = reduce_rel(dot(target_hidden, tgt_w_out))
         updated = (target_feat.astype(jnp.float32) + update).astype(jnp.bfloat16)
-        grad_source = last_step(counts_turned, back_near, back_far, slope, in_turned)
-        return (updated, grad_source[None])
+        grad_hidden = 0.0
+        for k in range(pairs):
+            for at, piece in ((k, back_near[k]), (pairs + k, back_far[k])):
+                grad_hidden = grad_hidden + dot(counts_turned[:, at * TILE : (at + 1) * TILE], piece)
+        grad_pre = (grad_hidden * slope).astype(jnp.bfloat16)
+        grad_source = dot(grad_pre, in_turned)
+        return (updated, grad_source.astype(jnp.bfloat16)[None])
 
     return shards
 

time: 129 us -> 125 us (0.969)
  local copies, waits for them, and re-layouts: 8.63 us -> 3.12 us
  matrix products: 14.2 us -> 16.7 us
  waiting for transfers between devices: 45.1 us -> 46.8 us
    dot_general x16 -> x24, matrix products: 12.1 us -> 16.7 us  [dot(): lax.dot_general(a, b, (((ca,), (cb,)), ((), ())), preferred_element_type=...]
    unnamed x72 -> x52, local copies, waits for them, and re-layouts: 4.9 us -> 2.08 us
    dot_general x1 -> x0, matrix products: 2.03 us -> none  [own_counts(): jnp.einsum('bet,bes->bts', target_hot, source_hot, preferred_element_type...]
    gather x3 -> x0, local copies, waits for them, and re-layouts: 1.78 us -> none  [the longest x1 0.65 us: shards(): columns = own_rows.reshape(rows, devs, shard)[:, order]]
    ppermute x43, waiting for transfers between devices: 45.1 us -> 46.8 us  [swap(): return lax.ppermute(value, axis, [(i, i ^ mask) for i in range(size)])]
    mul x2 -> x0, other arithmetic: 1.38 us -> none  [the longest x1 1.36 us: silu_slope(): return sigma * (1.0 + values * (1.0 - sigma))]
  transfers between devices with their start and end apart: 43 -> 43, of which waited for: 22 -> 21; matrix products, arithmetic and copies ran while one was open for 13% -> 7% of each run, Pallas kernels for 6% -> 9%
where the time goes in v3:
time: 125 us
  waiting for transfers between devices  46.8 us (37%)
  starting transfers between devices  43.3 us (35%)
  matrix products  16.7 us (13%)
  Pallas kernels  11.3 us (9%)
  local copies, waits for them, and re-layouts  3.12 us (2%)
  other arithmetic  2.7 us (2%)
    ppermute x43, waiting for transfers between devices, swap(): return lax.ppermute(value, axis, [(i, i ^ mask) for i in range(size)])  46.8 us
    ppermute x43, starting transfers between devices, swap(): return lax.ppermute(value, axis, [(i, i ^ mask) for i in range(size)])  43.3 us
    dot_general x24, matrix products, dot(): lax.dot_general(a, b, (((ca,), (cb,)), ((), ())), preferred_element_type=...  16.7 us
    pallas_call x3, Pallas kernels, call(): pl.pallas_call(body, out_shape=outs, in_specs=[pl.BlockSpec(memory_space=...  11.3 us
  transfers between devices with their start and end apart: 43, of which 21 were waited for; matrix products, arithmetic and copies ran while one was open for 7% of the time, Pallas kernels for 9%

profile of v3, /device:TPU:0, one launch (start us, length us, event | category | flops | bytes accessed | tf_op | source)
XLA Modules:
  0.0 125.1 jit_solution(14673654829125224613)
XLA Ops:
  1.2 2.6 %collective-permute-start.1 = (bf16[128,1024]{1,0:T(8,128)(2,1)}, bf16[128,1024]{1,0:T(8,128)(2,1)S(1)}, u32[]{:S(2)}, u32[]{:S(2)}) collective-permute-start(bf16[128,1024]{1,0:T(8,128)(2,1)} %bitcast.39), channel_id=1, source_target_pairs={{0,2},{1,3},{2,0},{3,1},{4,6},{5,7},{6,4},{7,5},{8,10},{9,11},{10,... | collective-permute-start | bytes 786440 | tf_op jit(solution)/shard_map/ppermute | solution.py:27
  5.9 3.6 %shard_map.122 = (bf16[1024,256]{1,0:T(8,128)(2,1)}, bf16[256,1024]{1,0:T(8,128)(2,1)}, bf16[256,1024]{1,0:T(8,128)(2,1)}) custom-call(s32[2]{0:T(128)} %pad_add_fusion.scalar_ref, s32[32]{0:T(128)} %bitcast.50, s32[32]{0:T(128)} %bitcast.51, s32[32,128]{1,0:T(8,128)} %bitcast.49, bf16[256,1024]{1,0:T(8,128)(2,1)} %bitcast.43), custom_call_target="tpu_custom_call" | custom-call | flops 1610612736 | bytes 2113800 | tf_op jit(solution)/shard_map/pallas_call | solution.py:33
  11.1 6.8 %collective-permute-done.3.refs_4_ = bf16[128,1024]{1,0:T(8,128)(2,1)S(1)} collective-permute-done((bf16[128,1024]{1,0:T(8,128)(2,1)}, bf16[128,1024]{1,0:T(8,128)(2,1)S(1)}, u32[]{:S(2)}, u32[]{:S(2)}) %collective-permute-start.3) | collective-permute-done | bytes 262176 | tf_op jit(solution)/shard_map/ppermute | solution.py:27
  25.8 2.6 %collective-permute-start.22 = (bf16[32,1024]{1,0:T(8,128)(2,1)S(1)}, bf16[32,1024]{1,0:T(8,128)(2,1)S(1)}, u32[]{:S(2)}, u32[]{:S(2)}) collective-permute-start(bf16[32,1024]{1,0:T(8,128)(2,1)S(1)} %copy-done.25), channel_id=1, source_target_pairs={{0,16},{8,24},{16,0},{24,8},{1,17},{9,25},{17,1},{25,9},{2,18},{10... | collective-permute-start | bytes 196616 | tf_op jit(solution)/shard_map/ppermute | solution.py:27
  28.6 2.0 %collective-permute-start.14 = (bf16[128,1024]{1,0:T(8,128)(2,1)S(1)}, bf16[128,1024]{1,0:T(8,128)(2,1)S(1)}, u32[]{:S(2)}, u32[]{:S(2)}) collective-permute-start(bf16[128,1024]{1,0:T(8,128)(2,1)S(1)} %bitcast.46), channel_id=1, source_target_pairs={{0,4},{1,5},{2,6},{3,7},{4,0},{5,1},{6,2},{7,3},{8,12},{9,13},{10,... | collective-permute-start | bytes 786440 | tf_op jit(solution)/shard_map/ppermute | solution.py:27
  30.7 2.8 %collective-permute-done.22 = bf16[32,1024]{1,0:T(8,128)(2,1)S(1)} collective-permute-done((bf16[32,1024]{1,0:T(8,128)(2,1)S(1)}, bf16[32,1024]{1,0:T(8,128)(2,1)S(1)}, u32[]{:S(2)}, u32[]{:S(2)}) %collective-permute-start.22) | collective-permute-done | bytes 65568 | tf_op jit(solution)/shard_map/ppermute | solution.py:27
  35.5 2.3 %collective-permute-done.12.refs_2_ = bf16[128,1024]{1,0:T(8,128)(2,1)S(1)} collective-permute-done((bf16[128,1024]{1,0:T(8,128)(2,1)S(1)}, bf16[128,1024]{1,0:T(8,128)(2,1)S(1)}, u32[]{:S(2)}, u32[]{:S(2)}) %collective-permute-start.12) | collective-permute-done | bytes 262176 | tf_op jit(solution)/shard_map/ppermute | solution.py:27
  37.8 3.6 %collective-permute-done.14.refs_4_ = bf16[128,1024]{1,0:T(8,128)(2,1)S(1)} collective-permute-done((bf16[128,1024]{1,0:T(8,128)(2,1)S(1)}, bf16[128,1024]{1,0:T(8,128)(2,1)S(1)}, u32[]{:S(2)}, u32[]{:S(2)}) %collective-permute-start.14) | collective-permute-done | bytes 262176 | tf_op jit(solution)/shard_map/ppermute | solution.py:27
  48.9 4.1 %shard_map.123 = (bf16[1024,1024]{1,0:T(8,128)(2,1)}, bf16[1024,1024]{1,0:T(8,128)(2,1)}) custom-call(s32[1]{0:T(128)} %bitcast.me_ref, bf16[128,1024]{1,0:T(8,128)(2,1)} %bitcast.44, bf16[128,1024]{1,0:T(8,128)(2,1)} %copy-done.22, bf16[128,1024]{1,0:T(8,128)(2,1)} %copy-done.19, bf16[128,1024]{1,0:T(8,128)(2,1)} %copy-done.23, ...), custom_call_target="tpu_custom_call" | custom-call | flops 4294967296 | bytes 6291460 | tf_op jit(solution)/shard_map/pallas_call | solution.py:33
  53.1 2.1 %collective-permute-done.10 = bf16[128,1024]{1,0:T(8,128)(2,1)} collective-permute-done((bf16[128,1024]{1,0:T(8,128)(2,1)}, bf16[128,1024]{1,0:T(8,128)(2,1)}, u32[]{:S(2)}, u32[]{:S(2)}) %collective-permute-start.10) | collective-permute-done | bytes 262176 | tf_op jit(solution)/shard_map/ppermute | solution.py:27
  55.2 4.5 %collective-permute-done.8 = bf16[128,1024]{1,0:T(8,128)(2,1)} collective-permute-done((bf16[128,1024]{1,0:T(8,128)(2,1)}, bf16[128,1024]{1,0:T(8,128)(2,1)}, u32[]{:S(2)}, u32[]{:S(2)}) %collective-permute-start.8) | collective-permute-done | bytes 262176 | tf_op jit(solution)/shard_map/ppermute | solution.py:27
  60.1 3.1 %fusion.76 = (bf16[128,1024]{1,0:T(8,128)(2,1)S(1)}, f32[128,1024]{1,0:T(8,128)}) fusion(bf16[1024,1024]{1,0:T(8,128)(2,1)} %get-tuple-element.15, f32[512,1024]{1,0:T(8,128)S(1)} %get-tuple-element.39, bf16[128,1024]{1,0:T(8,128)(2,1)} %collective-permute-done.10, bf16[128,1024]{1,0:T(8,128)(2,1)} %collective-permute-done.9, ...), kind=kOutput, calls=%fused_computation.104 | convolution fusion | flops 269484032 | bytes 4194304 | tf_op jit(solution)/shard_map/dot_general | solution.py:23
  64.2 3.2 %collective-permute-start.19 = (bf16[32,1024]{1,0:T(8,128)(2,1)S(1)}, bf16[32,1024]{1,0:T(8,128)(2,1)S(1)}, u32[]{:S(2)}, u32[]{:S(2)}) collective-permute-start(bf16[32,1024]{1,0:T(8,128)(2,1)S(1)} %get-tuple-element.37), channel_id=1, source_target_pairs={{0,16},{8,24},{16,0},{24,8},{1,17},{9,25},{17,1},{25,9},{2,18},{10... | collective-permute-start | bytes 196616 | tf_op jit(solution)/shard_map/ppermute | solution.py:27
  67.7 3.5 %shard_map.124 = bf16[1024,1024]{1,0:T(8,128)(2,1)} custom-call(s32[1]{0:T(128)} %bitcast.me_ref, bf16[128,1024]{1,0:T(8,128)(2,1)} %bitcast.42, bf16[128,1024]{1,0:T(8,128)(2,1)} %copy-done.8, bf16[128,1024]{1,0:T(8,128)(2,1)} %copy-done.9, bf16[128,1024]{1,0:T(8,128)(2,1)} %copy-done.13, bf16[128,1024]{1,0:T(8,128)(2,1)} %copy-done.11, ...), custom_call_target="tpu_custom_call" | custom-call | flops 2147483648 | bytes 4194308 | tf_op jit(solution)/shard_map/pallas_call | solution.py:33
  71.3 2.2 %collective-permute-done.20 = bf16[32,1024]{1,0:T(8,128)(2,1)S(1)} collective-permute-done((bf16[32,1024]{1,0:T(8,128)(2,1)S(1)}, bf16[32,1024]{1,0:T(8,128)(2,1)S(1)}, u32[]{:S(2)}, u32[]{:S(2)}) %collective-permute-start.20) | collective-permute-done | bytes 65568 | tf_op jit(solution)/shard_map/ppermute | solution.py:27
  79.2 2.6 %collective-permute-done.25 = bf16[32,1024]{1,0:T(8,128)(2,1)S(1)} collective-permute-done((bf16[32,1024]{1,0:T(8,128)(2,1)S(1)}, bf16[32,1024]{1,0:T(8,128)(2,1)S(1)}, u32[]{:S(2)}, u32[]{:S(2)}) %collective-permute-start.25) | collective-permute-done | bytes 65568 | tf_op jit(solution)/shard_map/ppermute | solution.py:27
  84.2 2.7 %collective-permute-start.28 = (bf16[32,1024]{1,0:T(8,128)(2,1)S(1)}, bf16[32,1024]{1,0:T(8,128)(2,1)S(1)}, u32[]{:S(2)}, u32[]{:S(2)}) collective-permute-start(bf16[32,1024]{1,0:T(8,128)(2,1)S(1)} %get-tuple-element.34), channel_id=1, source_target_pairs={{0,16},{8,24},{16,0},{24,8},{1,17},{9,25},{17,1},{25,9},{2,18},{10... | collective-permute-start | bytes 196616 | tf_op jit(solution)/shard_map/ppermute | solution.py:27
  89.9 3.7 %collective-permute-done.29 = bf16[32,1024]{1,0:T(8,128)(2,1)S(1)} collective-permute-done((bf16[32,1024]{1,0:T(8,128)(2,1)S(1)}, bf16[32,1024]{1,0:T(8,128)(2,1)S(1)}, u32[]{:S(2)}, u32[]{:S(2)}) %collective-permute-start.29) | collective-permute-done | bytes 65568 | tf_op jit(solution)/shard_map/ppermute | solution.py:27
  95.9 2.4 %collective-permute-start.32 = (bf16[32,1024]{1,0:T(8,128)(2,1)S(1)}, bf16[32,1024]{1,0:T(8,128)(2,1)S(1)}, u32[]{:S(2)}, u32[]{:S(2)}) collective-permute-start(bf16[32,1024]{1,0:T(8,128)(2,1)S(1)} %multiply_convert_fusion.4), channel_id=1, source_target_pairs={{0,24},{8,16},{16,8},{24,0},{1,25},{9,17},{17,9},{25,1},{2,26},{10... | collective-permute-start | bytes 196616 | tf_op jit(solution)/shard_map/ppermute | solution.py:27
  99.2 3.1 %collective-permute-done.32 = bf16[32,1024]{1,0:T(8,128)(2,1)S(1)} collective-permute-done((bf16[32,1024]{1,0:T(8,128)(2,1)S(1)}, bf16[32,1024]{1,0:T(8,128)(2,1)S(1)}, u32[]{:S(2)}, u32[]{:S(2)}) %collective-permute-start.32) | collective-permute-done | bytes 65568 | tf_op jit(solution)/shard_map/ppermute | solution.py:27
  105.6 3.1 %collective-permute-start.34 = (bf16[32,1024]{1,0:T(8,128)(2,1)S(1)}, bf16[32,1024]{1,0:T(8,128)(2,1)S(1)}, u32[]{:S(2)}, u32[]{:S(2)}) collective-permute-start(bf16[32,1024]{1,0:T(8,128)(2,1)S(1)} %get-tuple-element.31), channel_id=1, source_target_pairs={{0,16},{8,24},{16,0},{24,8},{1,17},{9,25},{17,1},{25,9},{2,18},{10... | collective-permute-start | bytes 196616 | tf_op jit(solution)/shard_map/ppermute | solution.py:27
  112.3 2.6 %collective-permute-done.35 = bf16[32,1024]{1,0:T(8,128)(2,1)S(1)} collective-permute-done((bf16[32,1024]{1,0:T(8,128)(2,1)S(1)}, bf16[32,1024]{1,0:T(8,128)(2,1)S(1)}, u32[]{:S(2)}, u32[]{:S(2)}) %collective-permute-start.35) | collective-permute-done | bytes 65568 | tf_op jit(solution)/shard_map/ppermute | solution.py:27
  116.9 3.1 %collective-permute-done.41 = bf16[128,1024]{1,0:T(8,128)(2,1)S(1)} collective-permute-done((bf16[128,1024]{1,0:T(8,128)(2,1)S(1)}, bf16[128,1024]{1,0:T(8,128)(2,1)S(1)}, u32[]{:S(2)}, u32[]{:S(2)}) %collective-permute-start.41) | collective-permute-done | bytes 262176 | tf_op jit(solution)/shard_map/ppermute | solution.py:27
  121.8 3.3 %fusion.6 = bf16[1,256,1024]{2,1,0:T(8,128)(2,1)} fusion(bf16[1024,1024]{1,0:T(8,128)(2,1)} %shard_map.124, f32[256,1024]{1,0:T(8,128)S(1)} %copy-done.2, f32[256,1024]{1,0:T(8,128)S(1)} %fusion.1, bf16[128,1024]{1,0:T(8,128)(2,1)S(1)} %collective-permute-done.42, bf16[256,1024]{1,0:T(8,128)(2,1)} %get-tuple-element.19), kind=kOutput, calls=%fused_computation.19 | convolution fusion | flops 605028352 | bytes 5046272 | tf_op jit(solution)/shard_map/dot_general | solution.py:23
  (155 shorter events, 48.1 us)
Async XLA Ops:
  0.6 18.5 %collective-permute-start = (bf16[128,1024]{1,0:T(8,128)(2,1)}, bf16[128,1024]{1,0:T(8,128)(2,1)S(1)}, u32[]{:S(2)}, u32[]{:S(2)}) collective-permute-start(bf16[128,1024]{1,0:T(8,128)(2,1)} %bitcast.38), channel_id=1, source_target_pairs={{0,1},{1,0},{2,3},{3,2},{4,5},{5,4},{6,7},{7,6},{8,9},{9,8},{10,11... | collective-permute-start | bytes 786440 | tf_op jit(solution)/shard_map/ppermute | solution.py:27
  1.2 9.9 %collective-permute-start.1 = (bf16[128,1024]{1,0:T(8,128)(2,1)}, bf16[128,1024]{1,0:T(8,128)(2,1)S(1)}, u32[]{:S(2)}, u32[]{:S(2)}) collective-permute-start(bf16[128,1024]{1,0:T(8,128)(2,1)} %bitcast.39), channel_id=1, source_target_pairs={{0,2},{1,3},{2,0},{3,1},{4,6},{5,7},{6,4},{7,5},{8,10},{9,11},{10,... | collective-permute-start | bytes 786440 | tf_op jit(solution)/shard_map/ppermute | solution.py:27
  3.8 14.2 %collective-permute-start.3 = (bf16[128,1024]{1,0:T(8,128)(2,1)}, bf16[128,1024]{1,0:T(8,128)(2,1)S(1)}, u32[]{:S(2)}, u32[]{:S(2)}) collective-permute-start(bf16[128,1024]{1,0:T(8,128)(2,1)} %bitcast.40), channel_id=1, source_target_pairs={{0,4},{1,5},{2,6},{3,7},{4,0},{5,1},{6,2},{7,3},{8,12},{9,13},{10,... | collective-permute-start | bytes 786440 | tf_op jit(solution)/shard_map/ppermute | solution.py:27
  5.3 14.6 %collective-permute-start.5 = (bf16[128,1024]{1,0:T(8,128)(2,1)}, bf16[128,1024]{1,0:T(8,128)(2,1)S(1)}, u32[]{:S(2)}, u32[]{:S(2)}) collective-permute-start(bf16[128,1024]{1,0:T(8,128)(2,1)} %bitcast.41), channel_id=1, source_target_pairs={{0,6},{1,7},{2,4},{3,5},{4,2},{5,3},{6,0},{7,1},{8,14},{9,15},{10,... | collective-permute-start | bytes 786440 | tf_op jit(solution)/shard_map/ppermute | solution.py:27
  11.1 9.5 %collective-permute-start.2 = (bf16[128,1024]{1,0:T(8,128)(2,1)S(1)}, bf16[128,1024]{1,0:T(8,128)(2,1)S(1)}, u32[]{:S(2)}, u32[]{:S(2)}) collective-permute-start(bf16[128,1024]{1,0:T(8,128)(2,1)S(1)} %collective-permute-done.1.refs_2_), channel_id=1, source_target_pairs={{0,1},{1,0},{2,3},{3,2},{4,5},{5,4},{6,7},{7,6},{8,9},{9,8},{10,11... | collective-permute-start | bytes 786440 | tf_op jit(solution)/shard_map/ppermute | solution.py:27
  24.0 19.0 %collective-permute-start.7 = (bf16[512,1024]{1,0:T(8,128)(2,1)S(1)}, bf16[512,1024]{1,0:T(8,128)(2,1)S(1)}, u32[]{:S(2)}, u32[]{:S(2)}) collective-permute-start(bf16[512,1024]{1,0:T(8,128)(2,1)S(1)} %convolution_convert_fusion), channel_id=1, source_target_pairs={{0,1},{1,0},{2,3},{3,2},{4,5},{5,4},{6,7},{7,6},{8,9},{9,8},{10,11... | collective-permute-start | bytes 3145736 | tf_op jit(solution)/shard_map/ppermute | solution.py:27
  25.8 7.7 %collective-permute-start.22 = (bf16[32,1024]{1,0:T(8,128)(2,1)S(1)}, bf16[32,1024]{1,0:T(8,128)(2,1)S(1)}, u32[]{:S(2)}, u32[]{:S(2)}) collective-permute-start(bf16[32,1024]{1,0:T(8,128)(2,1)S(1)} %copy-done.25), channel_id=1, source_target_pairs={{0,16},{8,24},{16,0},{24,8},{1,17},{9,25},{17,1},{25,9},{2,18},{10... | collective-permute-start | bytes 196616 | tf_op jit(solution)/shard_map/ppermute | solution.py:27
  28.4 6.6 %collective-permute-start.23 = (bf16[32,1024]{1,0:T(8,128)(2,1)S(1)}, bf16[32,1024]{1,0:T(8,128)(2,1)S(1)}, u32[]{:S(2)}, u32[]{:S(2)}) collective-permute-start(bf16[32,1024]{1,0:T(8,128)(2,1)S(1)} %copy-done.25), channel_id=1, source_target_pairs={{0,24},{8,16},{16,8},{24,0},{1,25},{9,17},{17,9},{25,1},{2,26},{10... | collective-permute-start | bytes 196616 | tf_op jit(solution)/shard_map/ppermute | solution.py:27
  28.6 9.2 %collective-permute-start.12 = (bf16[128,1024]{1,0:T(8,128)(2,1)S(1)}, bf16[128,1024]{1,0:T(8,128)(2,1)S(1)}, u32[]{:S(2)}, u32[]{:S(2)}) collective-permute-start(bf16[128,1024]{1,0:T(8,128)(2,1)S(1)} %bitcast.45), channel_id=1, source_target_pairs={{0,2},{1,3},{2,0},{3,1},{4,6},{5,7},{6,4},{7,5},{8,10},{9,11},{10,... | collective-permute-start | bytes 786440 | tf_op jit(solution)/shard_map/ppermute | solution.py:27
  28.6 12.8 %collective-permute-start.14 = (bf16[128,1024]{1,0:T(8,128)(2,1)S(1)}, bf16[128,1024]{1,0:T(8,128)(2,1)S(1)}, u32[]{:S(2)}, u32[]{:S(2)}) collective-permute-start(bf16[128,1024]{1,0:T(8,128)(2,1)S(1)} %bitcast.46), channel_id=1, source_target_pairs={{0,4},{1,5},{2,6},{3,7},{4,0},{5,1},{6,2},{7,3},{8,12},{9,13},{10,... | collective-permute-start | bytes 786440 | tf_op jit(solution)/shard_map/ppermute | solution.py:27
  33.5 9.6 %collective-permute-start.16 = (bf16[128,1024]{1,0:T(8,128)(2,1)S(1)}, bf16[128,1024]{1,0:T(8,128)(2,1)S(1)}, u32[]{:S(2)}, u32[]{:S(2)}) collective-permute-start(bf16[128,1024]{1,0:T(8,128)(2,1)S(1)} %bitcast.47), channel_id=1, source_target_pairs={{0,6},{1,7},{2,4},{3,5},{4,2},{5,3},{6,0},{7,1},{8,14},{9,15},{10,... | collective-permute-start | bytes 786440 | tf_op jit(solution)/shard_map/ppermute | solution.py:27
  35.0 11.8 %collective-permute-start.11 = (bf16[128,1024]{1,0:T(8,128)(2,1)S(1)}, bf16[128,1024]{1,0:T(8,128)(2,1)S(1)}, u32[]{:S(2)}, u32[]{:S(2)}) collective-permute-start(bf16[128,1024]{1,0:T(8,128)(2,1)S(1)} %bitcast.48), channel_id=1, source_target_pairs={{0,1},{1,0},{2,3},{3,2},{4,5},{5,4},{6,7},{7,6},{8,9},{9,8},{10,11... | collective-permute-start | bytes 786440 | tf_op jit(solution)/shard_map/ppermute | solution.py:27
  37.8 9.5 %collective-permute-start.13 = (bf16[128,1024]{1,0:T(8,128)(2,1)S(1)}, bf16[128,1024]{1,0:T(8,128)(2,1)S(1)}, u32[]{:S(2)}, u32[]{:S(2)}) collective-permute-start(bf16[128,1024]{1,0:T(8,128)(2,1)S(1)} %collective-permute-done.12.refs_2_), channel_id=1, source_target_pairs={{0,1},{1,0},{2,3},{3,2},{4,5},{5,4},{6,7},{7,6},{8,9},{9,8},{10,11... | collective-permute-start | bytes 786440 | tf_op jit(solution)/shard_map/ppermute | solution.py:27
  41.4 6.8 %collective-permute-start.15 = (bf16[128,1024]{1,0:T(8,128)(2,1)S(1)}, bf16[128,1024]{1,0:T(8,128)(2,1)S(1)}, u32[]{:S(2)}, u32[]{:S(2)}) collective-permute-start(bf16[128,1024]{1,0:T(8,128)(2,1)S(1)} %collective-permute-done.14.refs_4_), channel_id=1, source_target_pairs={{0,1},{1,0},{2,3},{3,2},{4,5},{5,4},{6,7},{7,6},{8,9},{9,8},{10,11... | collective-permute-start | bytes 786440 | tf_op jit(solution)/shard_map/ppermute | solution.py:27
  44.7 10.4 %collective-permute-start.10 = (bf16[128,1024]{1,0:T(8,128)(2,1)}, bf16[128,1024]{1,0:T(8,128)(2,1)}, u32[]{:S(2)}, u32[]{:S(2)}) collective-permute-start(bf16[128,1024]{1,0:T(8,128)(2,1)} %get-tuple-element.27), channel_id=1, source_target_pairs={{0,6},{1,7},{2,4},{3,5},{4,2},{5,3},{6,0},{7,1},{8,14},{9,15},{10,... | collective-permute-start | bytes 786440 | tf_op jit(solution)/shard_map/ppermute | solution.py:27
  46.8 12.9 %collective-permute-start.8 = (bf16[128,1024]{1,0:T(8,128)(2,1)}, bf16[128,1024]{1,0:T(8,128)(2,1)}, u32[]{:S(2)}, u32[]{:S(2)}) collective-permute-start(bf16[128,1024]{1,0:T(8,128)(2,1)} %get-tuple-element.26), channel_id=1, source_target_pairs={{0,2},{1,3},{2,0},{3,1},{4,6},{5,7},{6,4},{7,5},{8,10},{9,11},{10,... | collective-permute-start | bytes 786440 | tf_op jit(solution)/shard_map/ppermute | solution.py:27
  47.3 12.7 %collective-permute-start.9 = (bf16[128,1024]{1,0:T(8,128)(2,1)}, bf16[128,1024]{1,0:T(8,128)(2,1)}, u32[]{:S(2)}, u32[]{:S(2)}) collective-permute-start(bf16[128,1024]{1,0:T(8,128)(2,1)} %get-tuple-element.28), channel_id=1, source_target_pairs={{0,4},{1,5},{2,6},{3,7},{4,0},{5,1},{6,2},{7,3},{8,12},{9,13},{10,... | collective-permute-start | bytes 786440 | tf_op jit(solution)/shard_map/ppermute | solution.py:27
  63.2 8.0 %collective-permute-start.18 = (bf16[32,1024]{1,0:T(8,128)(2,1)S(1)}, bf16[32,1024]{1,0:T(8,128)(2,1)S(1)}, u32[]{:S(2)}, u32[]{:S(2)}) collective-permute-start(bf16[32,1024]{1,0:T(8,128)(2,1)S(1)} %get-tuple-element.35), channel_id=1, source_target_pairs={{0,8},{8,0},{16,24},{24,16},{1,9},{9,1},{17,25},{25,17},{2,10},{10... | collective-permute-start | bytes 196616 | tf_op jit(solution)/shard_map/ppermute | solution.py:27
  64.2 7.2 %collective-permute-start.19 = (bf16[32,1024]{1,0:T(8,128)(2,1)S(1)}, bf16[32,1024]{1,0:T(8,128)(2,1)S(1)}, u32[]{:S(2)}, u32[]{:S(2)}) collective-permute-start(bf16[32,1024]{1,0:T(8,128)(2,1)S(1)} %get-tuple-element.37), channel_id=1, source_target_pairs={{0,16},{8,24},{16,0},{24,8},{1,17},{9,25},{17,1},{25,9},{2,18},{10... | collective-permute-start | bytes 196616 | tf_op jit(solution)/shard_map/ppermute | solution.py:27
  75.4 6.4 %collective-permute-start.25 = (bf16[32,1024]{1,0:T(8,128)(2,1)S(1)}, bf16[32,1024]{1,0:T(8,128)(2,1)S(1)}, u32[]{:S(2)}, u32[]{:S(2)}) collective-permute-start(bf16[32,1024]{1,0:T(8,128)(2,1)S(1)} %multiply_convert_fusion.5), channel_id=1, source_target_pairs={{0,16},{8,24},{16,0},{24,8},{1,17},{9,25},{17,1},{25,9},{2,18},{10... | collective-permute-start | bytes 196616 | tf_op jit(solution)/shard_map/ppermute | solution.py:27
  86.9 6.7 %collective-permute-start.29 = (bf16[32,1024]{1,0:T(8,128)(2,1)S(1)}, bf16[32,1024]{1,0:T(8,128)(2,1)S(1)}, u32[]{:S(2)}, u32[]{:S(2)}) collective-permute-start(bf16[32,1024]{1,0:T(8,128)(2,1)S(1)} %get-tuple-element.33), channel_id=1, source_target_pairs={{0,24},{8,16},{16,8},{24,0},{1,25},{9,17},{17,9},{25,1},{2,26},{10... | collective-permute-start | bytes 196616 | tf_op jit(solution)/shard_map/ppermute | solution.py:27
  102.7 12.8 %collective-permute-start.37 = (bf16[128,1024]{1,0:T(8,128)(2,1)S(1)}, bf16[128,1024]{1,0:T(8,128)(2,1)S(1)}, u32[]{:S(2)}, u32[]{:S(2)}) collective-permute-start(bf16[128,1024]{1,0:T(8,128)(2,1)S(1)} %convolution_convert_fusion.2), channel_id=1, source_target_pairs={{0,2},{1,3},{2,0},{3,1},{4,6},{5,7},{6,4},{7,5},{8,10},{9,11},{10,... | collective-permute-start | bytes 786440 | tf_op jit(solution)/shard_map/ppermute | solution.py:27
  104.3 11.2 %collective-permute-start.39 = (bf16[128,1024]{1,0:T(8,128)(2,1)S(1)}, bf16[128,1024]{1,0:T(8,128)(2,1)S(1)}, u32[]{:S(2)}, u32[]{:S(2)}) collective-permute-start(bf16[128,1024]{1,0:T(8,128)(2,1)S(1)} %convolution_convert_fusion.2), channel_id=1, source_target_pairs={{0,4},{1,5},{2,6},{3,7},{4,0},{5,1},{6,2},{7,3},{8,12},{9,13},{10,... | collective-permute-start | bytes 786440 | tf_op jit(solution)/shard_map/ppermute | solution.py:27
  111.0 9.0 %collective-permute-start.41 = (bf16[128,1024]{1,0:T(8,128)(2,1)S(1)}, bf16[128,1024]{1,0:T(8,128)(2,1)S(1)}, u32[]{:S(2)}, u32[]{:S(2)}) collective-permute-start(bf16[128,1024]{1,0:T(8,128)(2,1)S(1)} %convolution_convert_fusion.2), channel_id=1, source_target_pairs={{0,6},{1,7},{2,4},{3,5},{4,2},{5,3},{6,0},{7,1},{8,14},{9,15},{10,... | collective-permute-start | bytes 786440 | tf_op jit(solution)/shard_map/ppermute | solution.py:27
  (45 other events, 308.1 us)

commit v4 on v3

--- a/solution.py
+++ b/solution.py
@@ -36,6 +36,7 @@
         in_specs=[pl.BlockSpec(memory_space=pltpu.SMEM)] * scalars
         + [pl.BlockSpec(memory_space=pltpu.VMEM)] * (len(operands) - scalars),
         out_specs=[pl.BlockSpec(memory_space=pltpu.VMEM)] * len(outs),
+        compiler_params=pltpu.CompilerParams(vmem_limit_bytes=16 << 20),
         cost_estimate=pl.CostEstimate(flops=flops, bytes_accessed=moved, transcendentals=0),
     )(*operands)
 
@@ -64,14 +65,14 @@
     return call(body, outs, [me[None]] + pieces, 1)
 
 
-def prepare(edge_codes, live_counts, source_ids, rows, me, turn, order, shard):
+def prepare(edge_codes, live_counts, source_ids, rows, me, turn, rels, order, shard):
     own, width = rows.shape
     slots = edge_codes.shape[1]
     count = len(order)
     inside = shard % LANES == 0
 
-    def body(scalar_ref, source_ref, live_ref, edge_ref, rows_ref, counts_ref, turned_ref, *rest):
-        at, twist = scalar_ref[0], scalar_ref[1]
+    def body(me_ref, turn_ref, source_ref, live_ref, edge_ref, rows_ref, counts_ref, turned_ref, *rest):
+        at, twist = me_ref[0], turn_ref[0] * (TILE // rels)
         slot = lax.broadcasted_iota(jnp.int32, (1, slots), 1)
         source_at = lax.broadcasted_iota(jnp.int32, (own, TILE_ROW * slots), 0)
         target_at = lax.broadcasted_iota(jnp.int32, (TILE, TILE_ROW * slots), 0)
@@ -99,8 +100,8 @@
         jax.ShapeDtypeStruct((own, count * TILE), jnp.bfloat16),
     ]
     outs += [jax.ShapeDtypeStruct((own, width), rows.dtype)] * inside
-    operands = [jnp.stack([me, turn]), source_ids, live_counts, edge_codes, rows]
-    results = call(body, outs, operands, 3)
+    operands = [me[None], turn[None], source_ids, live_counts, edge_codes, rows]
+    results = call(body, outs, operands, 4)
     if not inside:
         picked = jnp.asarray(order, jnp.int32) ^ me
         results = [*results, rows.reshape(own, count, shard)[:, picked].reshape(own, width)]
@@ -116,16 +117,22 @@
         near = [value] + [swap(value, "dev", devs, 2 * k) for k in range(1, pairs)]
         return near, [swap(piece, "dev", devs, 1) for piece in near]
 
-    def gather_rel(value):
-        return [value] + [swap(value, "rel", rels, q) for q in range(1, rels)]
-
-    def reduce_rel(value):
-        rows = value.shape[0] // rels
+    def gather_rel(value, masks=range(1, rels)):
+        return [value] + [swap(value, "rel", rels, q) for q in masks]
+
+    def reduce_rel(value, masks=range(1, rels)):
+        rows = value.shape[0] // (1 + len(masks))
         total = value[:rows]
-        for q in range(1, rels):
-            piece = value[q * rows : (q + 1) * rows].astype(jnp.bfloat16)
+        for i, q in enumerate(masks, 1):
+            piece = value[i * rows : (i + 1) * rows].astype(jnp.bfloat16)
             total = total + swap(piece, "rel", rels, q).astype(jnp.float32)
         return total
+
+    def from_partner(value, me, axis):
+        size = value.shape[axis] // 2
+        half = lax.dynamic_slice_in_dim(value, (me & 1) * size, size, axis)
+        near = swap(half, "rel", rels, 1)
+        return [near, swap(near, "dev", devs, 1)]
 
     def shards(
         src_feat,
@@ -148,14 +155,18 @@
 
         in_near, in_far = gather_dev(rel_w_in[0])
         out_near, out_far = gather_dev(rel_w_out[0])
-        shared_grad = gather_rel(out_grad)
+        evenly = range(2, rels, 2)
+        shared_grad = gather_rel(out_grad, evenly)
+        more_in = from_partner(tgt_w_in, me, 1)
+        more_out = from_partner(tgt_w_out, me, 0)
         counts, counts_turned, columns = prepare(
             tile_edges[0],
             tile_count[0],
             tile_source[0],
             own_rows,
             me,
-            rel * (TILE // rels),
+            rel,
+            rels,
             evens + odds,
             shard,
         )
@@ -167,26 +178,37 @@
 
         half = pairs * TILE
         far = swap(dot(counts[half:], hidden).astype(jnp.bfloat16), "dev", devs, 1)
+        hidden_pre, far = lax.optimization_barrier((hidden_pre, far))
+        slope = silu_slope(hidden_pre)
         near = dot(counts[:half], hidden) + far.astype(jnp.float32)
         total = near[:TILE]
         for k in range(1, pairs):
             piece = near[k * TILE : (k + 1) * TILE].astype(jnp.bfloat16)
             total = total + swap(piece, "dev", devs, 2 * k).astype(jnp.float32)
         out_full, out_turned = assemble(out_near, out_far, me, True, True)
-        agg = reduce_rel(dot(total.astype(jnp.bfloat16), out_full))
+        total, more_in, more_out = lax.optimization_barrier(
+            (total.astype(jnp.bfloat16), more_in, more_out)
+        )
+        agg = reduce_rel(dot(total, out_full))
 
         (in_turned,) = assemble(in_near, in_far, me, False, True)
-        slope = silu_slope(hidden_pre)
-        hidden_grad = dot(jnp.concatenate(shared_grad, 0), tgt_w_out, 1, 1)
-        agg, in_turned, slope, hidden_grad = lax.optimization_barrier(
-            (agg, in_turned, slope, hidden_grad)
+        tgt_in = [tgt_w_in, jnp.concatenate(more_in, 1)]
+        tgt_out = [tgt_w_out, jnp.concatenate(more_out, 0)]
+        shared_grad = jnp.concatenate(shared_grad, 0)
+        hidden_grad = [dot(shared_grad, weights, 1, 1) for weights in tgt_out]
+        agg, in_turned, slope, hidden_grad, tgt_in, tgt_out = lax.optimization_barrier(
+            (agg, in_turned, slope, hidden_grad, tgt_in, tgt_out)
         )
         inverse_norm = lax.rsqrt(jnp.mean(agg * agg, axis=1, keepdims=True) + eps_norm)
-        normed = gather_rel((agg * inverse_norm * gain).astype(jnp.bfloat16))
-        target_pre = dot(jnp.concatenate(normed, 0), tgt_w_in)
-        grad_pre_t = (hidden_grad * silu_slope(target_pre)).astype(jnp.bfloat16)
-        grad_normed = reduce_rel(dot(grad_pre_t, tgt_w_in, 1, 1))
-        target_hidden = jax.nn.silu(target_pre).astype(jnp.bfloat16)
+        normed = gather_rel((agg * inverse_norm * gain).astype(jnp.bfloat16), evenly)
+        normed = jnp.concatenate(normed, 0)
+        grad_normed, target_hidden = 0.0, []
+        for weights, above in zip(tgt_in, hidden_grad):
+            target_pre = dot(normed, weights)
+            grad_pre_t = (above * silu_slope(target_pre)).astype(jnp.bfloat16)
+            grad_normed = grad_normed + dot(grad_pre_t, weights, 1, 1)
+            target_hidden.append(jax.nn.silu(target_pre).astype(jnp.bfloat16))
+        grad_normed = reduce_rel(grad_normed, evenly)
         scaled = grad_normed * gain
         mean_term = jnp.mean(agg * scaled, axis=1, keepdims=True)
         grad_agg = inverse_norm * (scaled - agg * inverse_norm * inverse_norm * mean_term)
@@ -195,13 +217,14 @@
 
         back = dot(grad_agg, out_turned).astype(jnp.bfloat16)
         back_near, back_far = gather_dev(back)
-        update = reduce_rel(dot(target_hidden, tgt_w_out))
+        update = dot(target_hidden[0], tgt_out[0]) + dot(target_hidden[1], tgt_out[1])
+        update = reduce_rel(update, evenly)
         updated = (target_feat.astype(jnp.float32) + update).astype(jnp.bfloat16)
         grad_hidden = 0.0
         for k in range(pairs):
             for at, piece in ((k, back_near[k]), (pairs + k, back_far[k])):
                 grad_hidden = grad_hidden + dot(counts_turned[:, at * TILE : (at + 1) * TILE], piece)
-        grad_pre = (grad_hidden * slope).astype(jnp.bfloat16)
+        grad_pre = lax.optimization_barrier((grad_hidden * slope).astype(jnp.bfloat16))
         grad_source = dot(grad_pre, in_turned)
         return (updated, grad_source.astype(jnp.bfloat16)[None])
 

time: 125 us -> 118 us (0.944)
  waiting for transfers between devices: 46.8 us -> 55.8 us
  starting transfers between devices: 43.3 us -> 35.6 us
  Pallas kernels: 11.3 us -> 4.43 us
  matrix products: 16.7 us -> 14 us
  local copies, waits for them, and re-layouts: 3.12 us -> 4.68 us
    ppermute x43 -> x39, waiting for transfers between devices: 46.8 us -> 55.8 us  [swap(): return lax.ppermute(value, axis, [(i, i ^ mask) for i in range(size)])]
    ppermute x43 -> x39, starting transfers between devices: 43.3 us -> 35.6 us  [swap(): return lax.ppermute(value, axis, [(i, i ^ mask) for i in range(size)])]
    pallas_call x3, Pallas kernels: 11.3 us -> 4.43 us  [call(): pl.pallas_call(body, out_shape=outs, in_specs=[pl.BlockSpec(memory_space=...]
    dot_general x24 -> x29, matrix products: 16.7 us -> 14 us  [dot(): lax.dot_general(a, b, (((ca,), (cb,)), ((), ())), preferred_element_type=...]
    unnamed x52 -> x26, local copies, waits for them, and re-layouts: 2.08 us -> 3.15 us
  transfers between devices with their start and end apart: 43 -> 39, of which waited for: 21 -> 16; matrix products, arithmetic and copies ran while one was open for 7% -> 11% of each run, Pallas kernels for 9% -> 4%
where the time goes in v4:
time: 118 us
  waiting for transfers between devices  55.8 us (47%)
  starting transfers between devices  35.6 us (30%)
  matrix products  14 us (12%)
  local copies, waits for them, and re-layouts  4.68 us (4%)
  Pallas kernels  4.43 us (4%)
  other arithmetic  2.29 us (2%)
    ppermute x39, waiting for transfers between devices, swap(): return lax.ppermute(value, axis, [(i, i ^ mask) for i in range(size)])  55.8 us
    ppermute x39, starting transfers between devices, swap(): return lax.ppermute(value, axis, [(i, i ^ mask) for i in range(size)])  35.6 us
    dot_general x29, matrix products, dot(): lax.dot_general(a, b, (((ca,), (cb,)), ((), ())), preferred_element_type=...  14 us
    pallas_call x3, Pallas kernels, call(): pl.pallas_call(body, out_shape=outs, in_specs=[pl.BlockSpec(memory_space=...  4.43 us
    unnamed x26, local copies, waits for them, and re-layouts  3.15 us
  transfers between devices with their start and end apart: 39, of which 16 were waited for; matrix products, arithmetic and copies ran while one was open for 11% of the time, Pallas kernels for 4%

profile of v4, /device:TPU:0, one launch (start us, length us, event | category | flops | bytes accessed | tf_op | source)
XLA Modules:
  0.0 118.0 jit_solution(3399883244717201740)
XLA Ops:
  0.6 4.0 %collective-permute-start.5 = (bf16[128,1024]{1,0:T(8,128)(2,1)}, bf16[128,1024]{1,0:T(8,128)(2,1)}, u32[]{:S(2)}, u32[]{:S(2)}) collective-permute-start(bf16[128,1024]{1,0:T(8,128)(2,1)} %bitcast.47), channel_id=1, source_target_pairs={{0,6},{1,7},{2,4},{3,5},{4,2},{5,3},{6,0},{7,1},{8,14},{9,15},{10,... | collective-permute-start | bytes 786440 | tf_op jit(solution)/shard_map/ppermute | solution.py:27
  5.3 3.0 %collective-permute-start.25 = (bf16[32,1024]{1,0:T(8,128)(2,1)}, bf16[32,1024]{1,0:T(8,128)(2,1)S(1)}, u32[]{:S(2)}, u32[]{:S(2)}) collective-permute-start(bf16[32,1024]{1,0:T(8,128)(2,1)} %param.21), channel_id=1, source_target_pairs={{0,16},{8,24},{16,0},{24,8},{1,17},{9,25},{17,1},{25,9},{2,18},{10... | collective-permute-start | bytes 196616 | tf_op jit(solution)/shard_map/ppermute | solution.py:27
  11.3 2.0 %shard_map.122 = (bf16[1024,256]{1,0:T(8,128)(2,1)S(1)}, bf16[256,1024]{1,0:T(8,128)(2,1)S(1)}, bf16[256,1024]{1,0:T(8,128)(2,1)S(1)}) custom-call(s32[1]{0:T(128)} %bitcast.me_ref, s32[1]{0:T(128)} %bitcast.1.turn_ref, s32[32]{0:T(128)S(1)} %bitcast.59, s32[32]{0:T(128)S(1)} %bitcast.60, s32[32,128]{1,0:T(8,128)S(1)} %bitcast.58, bf16[256,1024]{1,0:T(8,128)(2,1)S(1)} %bitcast.52), custom_call_target="tpu_custom_call" | custom-call | flops 1610612736 | bytes 2113800 | tf_op jit(solution)/shard_map/pallas_call | solution.py:33
  16.0 1.6 %collective-permute-start.16 = (bf16[128,1024]{1,0:T(8,128)(2,1)S(1)}, bf16[128,1024]{1,0:T(8,128)(2,1)S(1)}, u32[]{:S(2)}, u32[]{:S(2)}) collective-permute-start(bf16[128,1024]{1,0:T(8,128)(2,1)S(1)} %bitcast.54), channel_id=1, source_target_pairs={{0,2},{1,3},{2,0},{3,1},{4,6},{5,7},{6,4},{7,5},{8,10},{9,11},{10,... | collective-permute-start | bytes 786440 | tf_op jit(solution)/shard_map/ppermute | solution.py:27
  17.8 1.6 %collective-permute-start.18 = (bf16[128,1024]{1,0:T(8,128)(2,1)S(1)}, bf16[128,1024]{1,0:T(8,128)(2,1)S(1)}, u32[]{:S(2)}, u32[]{:S(2)}) collective-permute-start(bf16[128,1024]{1,0:T(8,128)(2,1)S(1)} %bitcast.55), channel_id=1, source_target_pairs={{0,4},{1,5},{2,6},{3,7},{4,0},{5,1},{6,2},{7,3},{8,12},{9,13},{10,... | collective-permute-start | bytes 786440 | tf_op jit(solution)/shard_map/ppermute | solution.py:27
  26.5 1.6 %collective-permute-start.11 = (bf16[1024,256]{1,0:T(8,128)(2,1)S(1)}, bf16[1024,256]{1,0:T(8,128)(2,1)S(1)}, u32[]{:S(2)}, u32[]{:S(2)}) collective-permute-start(bf16[1024,256]{1,0:T(8,128)(2,1)S(1)} %constant_dynamic-slice_fusion.1), channel_id=1, source_target_pairs={{0,8},{8,0},{16,24},{24,16},{1,9},{9,1},{17,25},{25,17},{2,10},{10... | collective-permute-start | bytes 1572872 | tf_op jit(solution)/shard_map/ppermute | solution.py:27
  30.0 1.7 %shard_map.124 = bf16[1024,1024]{1,0:T(8,128)(2,1)S(1)} custom-call(s32[1]{0:T(128)} %bitcast.me_ref, bf16[128,1024]{1,0:T(8,128)(2,1)S(1)} %bitcast.51, bf16[128,1024]{1,0:T(8,128)(2,1)S(1)} %collective-permute-done.refs_1_, bf16[128,1024]{1,0:T(8,128)(2,1)S(1)} %collective-permute-done.1.refs_2_, bf16[128,1024]{1,0:T(8,128)(2,1)S(1)} %collective-permute-done.2.refs_3_, ...), custom_call_target="tpu_custom_call" | custom-call | flops 2147483648 | bytes 4194308 | tf_op jit(solution)/shard_map/pallas_call | solution.py:33
  32.4 8.9 %collective-permute-done.11 = bf16[1024,256]{1,0:T(8,128)(2,1)S(1)} collective-permute-done((bf16[1024,256]{1,0:T(8,128)(2,1)S(1)}, bf16[1024,256]{1,0:T(8,128)(2,1)S(1)}, u32[]{:S(2)}, u32[]{:S(2)}) %collective-permute-start.11) | collective-permute-done | bytes 524320 | tf_op jit(solution)/shard_map/ppermute | solution.py:27
  41.8 10.0 %collective-permute-done.13 = bf16[256,1024]{1,0:T(8,128)(2,1)S(1)} collective-permute-done((bf16[256,1024]{1,0:T(8,128)(2,1)S(1)}, bf16[256,1024]{1,0:T(8,128)(2,1)S(1)}, u32[]{:S(2)}, u32[]{:S(2)}) %collective-permute-start.13) | collective-permute-done | bytes 524320 | tf_op jit(solution)/shard_map/ppermute | solution.py:27
  53.7 2.4 %collective-permute-start.10 = (bf16[128,1024]{1,0:T(8,128)(2,1)S(1)}, bf16[128,1024]{1,0:T(8,128)(2,1)S(1)}, u32[]{:S(2)}, u32[]{:S(2)}) collective-permute-start(bf16[128,1024]{1,0:T(8,128)(2,1)S(1)} %get-tuple-element.53), channel_id=1, source_target_pairs={{0,6},{1,7},{2,4},{3,5},{4,2},{5,3},{6,0},{7,1},{8,14},{9,15},{10,... | collective-permute-start | bytes 786440 | tf_op jit(solution)/shard_map/ppermute | solution.py:27
  57.6 6.3 %collective-permute-done.10 = bf16[128,1024]{1,0:T(8,128)(2,1)S(1)} collective-permute-done((bf16[128,1024]{1,0:T(8,128)(2,1)S(1)}, bf16[128,1024]{1,0:T(8,128)(2,1)S(1)}, u32[]{:S(2)}, u32[]{:S(2)}) %collective-permute-start.10) | collective-permute-done | bytes 262176 | tf_op jit(solution)/shard_map/ppermute | solution.py:27
  63.9 4.6 %collective-permute-done.9 = bf16[128,1024]{1,0:T(8,128)(2,1)S(1)} collective-permute-done((bf16[128,1024]{1,0:T(8,128)(2,1)S(1)}, bf16[128,1024]{1,0:T(8,128)(2,1)S(1)}, u32[]{:S(2)}, u32[]{:S(2)}) %collective-permute-start.9) | collective-permute-done | bytes 262176 | tf_op jit(solution)/shard_map/ppermute | solution.py:27
  69.2 3.0 %collective-permute-start.24 = (bf16[32,1024]{1,0:T(8,128)(2,1)S(1)}, bf16[32,1024]{1,0:T(8,128)(2,1)S(1)}, u32[]{:S(2)}, u32[]{:S(2)}) collective-permute-start(bf16[32,1024]{1,0:T(8,128)(2,1)S(1)} %get-tuple-element.56), channel_id=1, source_target_pairs={{0,24},{8,16},{16,8},{24,0},{1,25},{9,17},{17,9},{25,1},{2,26},{10... | collective-permute-start | bytes 196616 | tf_op jit(solution)/shard_map/ppermute | solution.py:27
  74.3 1.6 %collective-permute-done.24 = bf16[32,1024]{1,0:T(8,128)(2,1)S(1)} collective-permute-done((bf16[32,1024]{1,0:T(8,128)(2,1)S(1)}, bf16[32,1024]{1,0:T(8,128)(2,1)S(1)}, u32[]{:S(2)}, u32[]{:S(2)}) %collective-permute-start.24) | collective-permute-done | bytes 65568 | tf_op jit(solution)/shard_map/ppermute | solution.py:27
  75.9 2.7 %collective-permute-done.23 = bf16[32,1024]{1,0:T(8,128)(2,1)S(1)} collective-permute-done((bf16[32,1024]{1,0:T(8,128)(2,1)S(1)}, bf16[32,1024]{1,0:T(8,128)(2,1)S(1)}, u32[]{:S(2)}, u32[]{:S(2)}) %collective-permute-start.23) | collective-permute-done | bytes 65568 | tf_op jit(solution)/shard_map/ppermute | solution.py:27
  79.8 4.4 %collective-permute-done.26 = bf16[32,1024]{1,0:T(8,128)(2,1)S(1)} collective-permute-done((bf16[32,1024]{1,0:T(8,128)(2,1)S(1)}, bf16[32,1024]{1,0:T(8,128)(2,1)S(1)}, u32[]{:S(2)}, u32[]{:S(2)}) %collective-permute-start.26) | collective-permute-done | bytes 65568 | tf_op jit(solution)/shard_map/ppermute | solution.py:27
  86.6 5.2 %collective-permute-done.27 = bf16[32,1024]{1,0:T(8,128)(2,1)S(1)} collective-permute-done((bf16[32,1024]{1,0:T(8,128)(2,1)S(1)}, bf16[32,1024]{1,0:T(8,128)(2,1)S(1)}, u32[]{:S(2)}, u32[]{:S(2)}) %collective-permute-start.27) | collective-permute-done | bytes 65568 | tf_op jit(solution)/shard_map/ppermute | solution.py:27
  92.0 2.4 %collective-permute-start.30 = (bf16[32,1024]{1,0:T(8,128)(2,1)S(1)}, bf16[32,1024]{1,0:T(8,128)(2,1)S(1)}, u32[]{:S(2)}, u32[]{:S(2)}) collective-permute-start(bf16[32,1024]{1,0:T(8,128)(2,1)S(1)} %multiply_convert_fusion.1), channel_id=1, source_target_pairs={{0,24},{8,16},{16,8},{24,0},{1,25},{9,17},{17,9},{25,1},{2,26},{10... | collective-permute-start | bytes 196616 | tf_op jit(solution)/shard_map/ppermute | solution.py:27
  94.3 2.1 %collective-permute-start.28 = (bf16[32,1024]{1,0:T(8,128)(2,1)S(1)}, bf16[32,1024]{1,0:T(8,128)(2,1)S(1)}, u32[]{:S(2)}, u32[]{:S(2)}) collective-permute-start(bf16[32,1024]{1,0:T(8,128)(2,1)S(1)} %multiply_convert_fusion.1), channel_id=1, source_target_pairs={{0,8},{8,0},{16,24},{24,16},{1,9},{9,1},{17,25},{25,17},{2,10},{10... | collective-permute-start | bytes 196616 | tf_op jit(solution)/shard_map/ppermute | solution.py:27
  96.4 1.7 %collective-permute-done.30 = bf16[32,1024]{1,0:T(8,128)(2,1)S(1)} collective-permute-done((bf16[32,1024]{1,0:T(8,128)(2,1)S(1)}, bf16[32,1024]{1,0:T(8,128)(2,1)S(1)}, u32[]{:S(2)}, u32[]{:S(2)}) %collective-permute-start.30) | collective-permute-done | bytes 65568 | tf_op jit(solution)/shard_map/ppermute | solution.py:27
  100.0 1.6 %collective-permute-start.37 = (bf16[128,1024]{1,0:T(8,128)(2,1)S(1)}, bf16[128,1024]{1,0:T(8,128)(2,1)S(1)}, u32[]{:S(2)}, u32[]{:S(2)}) collective-permute-start(bf16[128,1024]{1,0:T(8,128)(2,1)S(1)} %convolution_convert_fusion.2), channel_id=1, source_target_pairs={{0,6},{1,7},{2,4},{3,5},{4,2},{5,3},{6,0},{7,1},{8,14},{9,15},{10,... | collective-permute-start | bytes 786440 | tf_op jit(solution)/shard_map/ppermute | solution.py:27
  101.6 1.8 %collective-permute-start.35 = (bf16[128,1024]{1,0:T(8,128)(2,1)S(1)}, bf16[128,1024]{1,0:T(8,128)(2,1)S(1)}, u32[]{:S(2)}, u32[]{:S(2)}) collective-permute-start(bf16[128,1024]{1,0:T(8,128)(2,1)S(1)} %convolution_convert_fusion.2), channel_id=1, source_target_pairs={{0,4},{1,5},{2,6},{3,7},{4,0},{5,1},{6,2},{7,3},{8,12},{9,13},{10,... | collective-permute-start | bytes 786440 | tf_op jit(solution)/shard_map/ppermute | solution.py:27
  104.4 2.1 %collective-permute-start.31 = (bf16[32,1024]{1,0:T(8,128)(2,1)S(1)}, bf16[32,1024]{1,0:T(8,128)(2,1)S(1)}, u32[]{:S(2)}, u32[]{:S(2)}) collective-permute-start(bf16[32,1024]{1,0:T(8,128)(2,1)S(1)} %slice.202), channel_id=1, source_target_pairs={{0,16},{8,24},{16,0},{24,8},{1,17},{9,25},{17,1},{25,9},{2,18},{10... | collective-permute-start | bytes 196616 | tf_op jit(solution)/shard_map/ppermute | solution.py:27
  106.8 4.4 %collective-permute-done.31 = bf16[32,1024]{1,0:T(8,128)(2,1)S(1)} collective-permute-done((bf16[32,1024]{1,0:T(8,128)(2,1)S(1)}, bf16[32,1024]{1,0:T(8,128)(2,1)S(1)}, u32[]{:S(2)}, u32[]{:S(2)}) %collective-permute-start.31) | collective-permute-done | bytes 65568 | tf_op jit(solution)/shard_map/ppermute | solution.py:27
  (133 shorter events, 36.3 us)
Async XLA Ops:
  0.6 19.1 %collective-permute-start.5 = (bf16[128,1024]{1,0:T(8,128)(2,1)}, bf16[128,1024]{1,0:T(8,128)(2,1)}, u32[]{:S(2)}, u32[]{:S(2)}) collective-permute-start(bf16[128,1024]{1,0:T(8,128)(2,1)} %bitcast.47), channel_id=1, source_target_pairs={{0,6},{1,7},{2,4},{3,5},{4,2},{5,3},{6,0},{7,1},{8,14},{9,15},{10,... | collective-permute-start | bytes 786440 | tf_op jit(solution)/shard_map/ppermute | solution.py:27
  4.6 16.4 %collective-permute-start.3 = (bf16[128,1024]{1,0:T(8,128)(2,1)}, bf16[128,1024]{1,0:T(8,128)(2,1)}, u32[]{:S(2)}, u32[]{:S(2)}) collective-permute-start(bf16[128,1024]{1,0:T(8,128)(2,1)} %bitcast.48), channel_id=1, source_target_pairs={{0,4},{1,5},{2,6},{3,7},{4,0},{5,1},{6,2},{7,3},{8,12},{9,13},{10,... | collective-permute-start | bytes 786440 | tf_op jit(solution)/shard_map/ppermute | solution.py:27
  5.1 10.8 %collective-permute-start = (bf16[128,1024]{1,0:T(8,128)(2,1)}, bf16[128,1024]{1,0:T(8,128)(2,1)S(1)}, u32[]{:S(2)}, u32[]{:S(2)}) collective-permute-start(bf16[128,1024]{1,0:T(8,128)(2,1)} %bitcast.49), channel_id=1, source_target_pairs={{0,1},{1,0},{2,3},{3,2},{4,5},{5,4},{6,7},{7,6},{8,9},{9,8},{10,11... | collective-permute-start | bytes 786440 | tf_op jit(solution)/shard_map/ppermute | solution.py:27
  5.1 12.7 %collective-permute-start.1 = (bf16[128,1024]{1,0:T(8,128)(2,1)}, bf16[128,1024]{1,0:T(8,128)(2,1)S(1)}, u32[]{:S(2)}, u32[]{:S(2)}) collective-permute-start(bf16[128,1024]{1,0:T(8,128)(2,1)} %bitcast.50), channel_id=1, source_target_pairs={{0,2},{1,3},{2,0},{3,1},{4,6},{5,7},{6,4},{7,5},{8,10},{9,11},{10,... | collective-permute-start | bytes 786440 | tf_op jit(solution)/shard_map/ppermute | solution.py:27
  5.3 10.6 %collective-permute-start.25 = (bf16[32,1024]{1,0:T(8,128)(2,1)}, bf16[32,1024]{1,0:T(8,128)(2,1)S(1)}, u32[]{:S(2)}, u32[]{:S(2)}) collective-permute-start(bf16[32,1024]{1,0:T(8,128)(2,1)} %param.21), channel_id=1, source_target_pairs={{0,16},{8,24},{16,0},{24,8},{1,17},{9,25},{17,1},{25,9},{2,18},{10... | collective-permute-start | bytes 196616 | tf_op jit(solution)/shard_map/ppermute | solution.py:27
  15.9 13.1 %collective-permute-start.15 = (bf16[128,1024]{1,0:T(8,128)(2,1)S(1)}, bf16[128,1024]{1,0:T(8,128)(2,1)S(1)}, u32[]{:S(2)}, u32[]{:S(2)}) collective-permute-start(bf16[128,1024]{1,0:T(8,128)(2,1)S(1)} %bitcast.53), channel_id=1, source_target_pairs={{0,1},{1,0},{2,3},{3,2},{4,5},{5,4},{6,7},{7,6},{8,9},{9,8},{10,11... | collective-permute-start | bytes 786440 | tf_op jit(solution)/shard_map/ppermute | solution.py:27
  16.0 13.5 %collective-permute-start.16 = (bf16[128,1024]{1,0:T(8,128)(2,1)S(1)}, bf16[128,1024]{1,0:T(8,128)(2,1)S(1)}, u32[]{:S(2)}, u32[]{:S(2)}) collective-permute-start(bf16[128,1024]{1,0:T(8,128)(2,1)S(1)} %bitcast.54), channel_id=1, source_target_pairs={{0,2},{1,3},{2,0},{3,1},{4,6},{5,7},{6,4},{7,5},{8,10},{9,11},{10,... | collective-permute-start | bytes 786440 | tf_op jit(solution)/shard_map/ppermute | solution.py:27
  17.8 14.1 %collective-permute-start.18 = (bf16[128,1024]{1,0:T(8,128)(2,1)S(1)}, bf16[128,1024]{1,0:T(8,128)(2,1)S(1)}, u32[]{:S(2)}, u32[]{:S(2)}) collective-permute-start(bf16[128,1024]{1,0:T(8,128)(2,1)S(1)} %bitcast.55), channel_id=1, source_target_pairs={{0,4},{1,5},{2,6},{3,7},{4,0},{5,1},{6,2},{7,3},{8,12},{9,13},{10,... | collective-permute-start | bytes 786440 | tf_op jit(solution)/shard_map/ppermute | solution.py:27
  21.0 11.2 %collective-permute-start.20 = (bf16[128,1024]{1,0:T(8,128)(2,1)S(1)}, bf16[128,1024]{1,0:T(8,128)(2,1)S(1)}, u32[]{:S(2)}, u32[]{:S(2)}) collective-permute-start(bf16[128,1024]{1,0:T(8,128)(2,1)S(1)} %bitcast.56), channel_id=1, source_target_pairs={{0,6},{1,7},{2,4},{3,5},{4,2},{5,3},{6,0},{7,1},{8,14},{9,15},{10,... | collective-permute-start | bytes 786440 | tf_op jit(solution)/shard_map/ppermute | solution.py:27
  26.5 14.8 %collective-permute-start.11 = (bf16[1024,256]{1,0:T(8,128)(2,1)S(1)}, bf16[1024,256]{1,0:T(8,128)(2,1)S(1)}, u32[]{:S(2)}, u32[]{:S(2)}) collective-permute-start(bf16[1024,256]{1,0:T(8,128)(2,1)S(1)} %constant_dynamic-slice_fusion.1), channel_id=1, source_target_pairs={{0,8},{8,0},{16,24},{24,16},{1,9},{9,1},{17,25},{25,17},{2,10},{10... | collective-permute-start | bytes 1572872 | tf_op jit(solution)/shard_map/ppermute | solution.py:27
  29.0 22.8 %collective-permute-start.13 = (bf16[256,1024]{1,0:T(8,128)(2,1)S(1)}, bf16[256,1024]{1,0:T(8,128)(2,1)S(1)}, u32[]{:S(2)}, u32[]{:S(2)}) collective-permute-start(bf16[256,1024]{1,0:T(8,128)(2,1)S(1)} %constant_dynamic-slice_fusion), channel_id=1, source_target_pairs={{0,8},{8,0},{16,24},{24,16},{1,9},{9,1},{17,25},{25,17},{2,10},{10... | collective-permute-start | bytes 1572872 | tf_op jit(solution)/shard_map/ppermute | solution.py:27
  29.5 23.6 %collective-permute-start.7 = (bf16[512,1024]{1,0:T(8,128)(2,1)S(1)}, bf16[512,1024]{1,0:T(8,128)(2,1)S(1)}, u32[]{:S(2)}, u32[]{:S(2)}) collective-permute-start(bf16[512,1024]{1,0:T(8,128)(2,1)S(1)} %convolution_convert_fusion), channel_id=1, source_target_pairs={{0,1},{1,0},{2,3},{3,2},{4,5},{5,4},{6,7},{7,6},{8,9},{9,8},{10,11... | collective-permute-start | bytes 3145736 | tf_op jit(solution)/shard_map/ppermute | solution.py:27
  31.9 19.9 %collective-permute-start.17 = (bf16[128,1024]{1,0:T(8,128)(2,1)S(1)}, bf16[128,1024]{1,0:T(8,128)(2,1)S(1)}, u32[]{:S(2)}, u32[]{:S(2)}) collective-permute-start(bf16[128,1024]{1,0:T(8,128)(2,1)S(1)} %collective-permute-done.16.refs_2_), channel_id=1, source_target_pairs={{0,1},{1,0},{2,3},{3,2},{4,5},{5,4},{6,7},{7,6},{8,9},{9,8},{10,11... | collective-permute-start | bytes 786440 | tf_op jit(solution)/shard_map/ppermute | solution.py:27
  32.3 20.0 %collective-permute-start.19 = (bf16[128,1024]{1,0:T(8,128)(2,1)S(1)}, bf16[128,1024]{1,0:T(8,128)(2,1)S(1)}, u32[]{:S(2)}, u32[]{:S(2)}) collective-permute-start(bf16[128,1024]{1,0:T(8,128)(2,1)S(1)} %collective-permute-done.18.refs_4_), channel_id=1, source_target_pairs={{0,1},{1,0},{2,3},{3,2},{4,5},{5,4},{6,7},{7,6},{8,9},{9,8},{10,11... | collective-permute-start | bytes 786440 | tf_op jit(solution)/shard_map/ppermute | solution.py:27
  41.3 11.0 %collective-permute-start.21 = (bf16[128,1024]{1,0:T(8,128)(2,1)S(1)}, bf16[128,1024]{1,0:T(8,128)(2,1)S(1)}, u32[]{:S(2)}, u32[]{:S(2)}) collective-permute-start(bf16[128,1024]{1,0:T(8,128)(2,1)S(1)} %collective-permute-done.20.refs_6_), channel_id=1, source_target_pairs={{0,1},{1,0},{2,3},{3,2},{4,5},{5,4},{6,7},{7,6},{8,9},{9,8},{10,11... | collective-permute-start | bytes 786440 | tf_op jit(solution)/shard_map/ppermute | solution.py:27
  51.8 16.9 %collective-permute-start.12 = (bf16[1024,256]{1,0:T(8,128)(2,1)S(1)}, bf16[1024,256]{1,0:T(8,128)(2,1)S(1)}, u32[]{:S(2)}, u32[]{:S(2)}) collective-permute-start(bf16[1024,256]{1,0:T(8,128)(2,1)S(1)} %collective-permute-done.11), channel_id=1, source_target_pairs={{0,1},{1,0},{2,3},{3,2},{4,5},{5,4},{6,7},{7,6},{8,9},{9,8},{10,11... | collective-permute-start | bytes 1572872 | tf_op jit(solution)/shard_map/ppermute | solution.py:27
  51.8 16.9 %collective-permute-start.14 = (bf16[256,1024]{1,0:T(8,128)(2,1)S(1)}, bf16[256,1024]{1,0:T(8,128)(2,1)S(1)}, u32[]{:S(2)}, u32[]{:S(2)}) collective-permute-start(bf16[256,1024]{1,0:T(8,128)(2,1)S(1)} %collective-permute-done.13), channel_id=1, source_target_pairs={{0,1},{1,0},{2,3},{3,2},{4,5},{5,4},{6,7},{7,6},{8,9},{9,8},{10,11... | collective-permute-start | bytes 1572872 | tf_op jit(solution)/shard_map/ppermute | solution.py:27
  53.7 10.2 %collective-permute-start.10 = (bf16[128,1024]{1,0:T(8,128)(2,1)S(1)}, bf16[128,1024]{1,0:T(8,128)(2,1)S(1)}, u32[]{:S(2)}, u32[]{:S(2)}) collective-permute-start(bf16[128,1024]{1,0:T(8,128)(2,1)S(1)} %get-tuple-element.53), channel_id=1, source_target_pairs={{0,6},{1,7},{2,4},{3,5},{4,2},{5,3},{6,0},{7,1},{8,14},{9,15},{10,... | collective-permute-start | bytes 786440 | tf_op jit(solution)/shard_map/ppermute | solution.py:27
  56.1 12.4 %collective-permute-start.9 = (bf16[128,1024]{1,0:T(8,128)(2,1)S(1)}, bf16[128,1024]{1,0:T(8,128)(2,1)S(1)}, u32[]{:S(2)}, u32[]{:S(2)}) collective-permute-start(bf16[128,1024]{1,0:T(8,128)(2,1)S(1)} %get-tuple-element.54), channel_id=1, source_target_pairs={{0,4},{1,5},{2,6},{3,7},{4,0},{5,1},{6,2},{7,3},{8,12},{9,13},{10,... | collective-permute-start | bytes 786440 | tf_op jit(solution)/shard_map/ppermute | solution.py:27
  56.6 11.9 %collective-permute-start.8 = (bf16[128,1024]{1,0:T(8,128)(2,1)S(1)}, bf16[128,1024]{1,0:T(8,128)(2,1)S(1)}, u32[]{:S(2)}, u32[]{:S(2)}) collective-permute-start(bf16[128,1024]{1,0:T(8,128)(2,1)S(1)} %get-tuple-element.52), channel_id=1, source_target_pairs={{0,2},{1,3},{2,0},{3,1},{4,6},{5,7},{6,4},{7,5},{8,10},{9,11},{10,... | collective-permute-start | bytes 786440 | tf_op jit(solution)/shard_map/ppermute | solution.py:27
  100.0 12.8 %collective-permute-start.37 = (bf16[128,1024]{1,0:T(8,128)(2,1)S(1)}, bf16[128,1024]{1,0:T(8,128)(2,1)S(1)}, u32[]{:S(2)}, u32[]{:S(2)}) collective-permute-start(bf16[128,1024]{1,0:T(8,128)(2,1)S(1)} %convolution_convert_fusion.2), channel_id=1, source_target_pairs={{0,6},{1,7},{2,4},{3,5},{4,2},{5,3},{6,0},{7,1},{8,14},{9,15},{10,... | collective-permute-start | bytes 786440 | tf_op jit(solution)/shard_map/ppermute | solution.py:27
  101.6 12.6 %collective-permute-start.35 = (bf16[128,1024]{1,0:T(8,128)(2,1)S(1)}, bf16[128,1024]{1,0:T(8,128)(2,1)S(1)}, u32[]{:S(2)}, u32[]{:S(2)}) collective-permute-start(bf16[128,1024]{1,0:T(8,128)(2,1)S(1)} %convolution_convert_fusion.2), channel_id=1, source_target_pairs={{0,4},{1,5},{2,6},{3,7},{4,0},{5,1},{6,2},{7,3},{8,12},{9,13},{10,... | collective-permute-start | bytes 786440 | tf_op jit(solution)/shard_map/ppermute | solution.py:27
  103.4 10.1 %collective-permute-start.32 = (bf16[128,1024]{1,0:T(8,128)(2,1)S(1)}, bf16[128,1024]{1,0:T(8,128)(2,1)S(1)}, u32[]{:S(2)}, u32[]{:S(2)}) collective-permute-start(bf16[128,1024]{1,0:T(8,128)(2,1)S(1)} %convolution_convert_fusion.2), channel_id=1, source_target_pairs={{0,1},{1,0},{2,3},{3,2},{4,5},{5,4},{6,7},{7,6},{8,9},{9,8},{10,11... | collective-permute-start | bytes 786440 | tf_op jit(solution)/shard_map/ppermute | solution.py:27
  103.4 9.3 %collective-permute-start.33 = (bf16[128,1024]{1,0:T(8,128)(2,1)S(1)}, bf16[128,1024]{1,0:T(8,128)(2,1)S(1)}, u32[]{:S(2)}, u32[]{:S(2)}) collective-permute-start(bf16[128,1024]{1,0:T(8,128)(2,1)S(1)} %convolution_convert_fusion.2), channel_id=1, source_target_pairs={{0,2},{1,3},{2,0},{3,1},{4,6},{5,7},{6,4},{7,5},{8,10},{9,11},{10,... | collective-permute-start | bytes 786440 | tf_op jit(solution)/shard_map/ppermute | solution.py:27
  (27 other events, 113.4 us)
